TPU v7x, 256 devices: a whole 4x4x8 slice. The times are simulated.
256 devices in a mesh: expert: 8 (over y_lo, x), fsdp: 32 (over y_hi, z, core).
Axes of the slice: x: 4, y: 4 (y_hi: 2, y_lo: 2; y = y_hi * 2 + y_lo), z: 8, core: 2. Of those that a mesh axis runs over, the one named last changes fastest.
Arguments:
- tokens: bfloat16 [1024, 3072], P('expert'), may hold values from -6 to 6
- assignment: int32 [1024, 2], P('expert'), may hold values from 0 to 7, all different within a row; in each aligned block of 128 rows (0 to 127, 128 to 255, ...) at most 48 rows name the same one
- route_weight: float32 [1024, 2], P('expert'), may hold values from 0.25 to 1
- cotangent: bfloat16 [1024, 3072], P('expert'), may hold values from -6 to 6
- w_gate: bfloat16 [8, 3072, 8192], P('expert', None, 'fsdp'), may hold values from -0.109375 to 0.109375
- w_up: bfloat16 [8, 3072, 8192], P('expert', None, 'fsdp'), may hold values from -0.109375 to 0.109375
- w_down: bfloat16 [8, 8192, 3072], P('expert', 'fsdp'), may hold values from -0.0625 to 0.0625
Outputs:
- moe_out: bfloat16 [1024, 3072], P('expert')
- grad_tokens: bfloat16 [1024, 3072], P('expert')
- grad_prob: float32 [1024, 2], P('expert')
- grad_gate: bfloat16 [8, 3072, 8192], P('expert', None, 'fsdp')
- grad_up: bfloat16 [8, 3072, 8192], P('expert', None, 'fsdp')
- grad_down: bfloat16 [8, 8192, 3072], P('expert', 'fsdp')
Inputs may be any that keep to these rules, and one draw needn't show every extreme that they name: `assignment`: each token names two different experts. Among the 128 tokens of one block no expert is named more than 48 times, and in some block some expert is named exactly 48 times.
All inputs are finite; a program needn't handle non-finite values.
Results may differ from a plain program's by a relative error of at most 0.02.
Values may be sent and summed in bfloat16 or wider, within the bound.
A program may use at most 128 MiB of HBM per device.

v0:
```python
import jax
import jax.numpy as jnp
from jax import lax
from jax.sharding import PartitionSpec as P


def slot_table(assignment, groups, capacity):
    flat = assignment.reshape(-1)
    onehot = (flat[:, None] == jnp.arange(groups, dtype=jnp.int32)[None, :]).astype(jnp.int32)
    before = jnp.cumsum(onehot, axis=0) - onehot
    position = jnp.sum(before * onehot, axis=1)
    return (flat * capacity + position).reshape(assignment.shape)


def front_half(gathered, gate_local, up_local):
    pre_gate = jnp.dot(gathered, gate_local, preferred_element_type=jnp.float32)
    pre_up = jnp.dot(gathered, up_local, preferred_element_type=jnp.float32)
    sigma = jax.nn.sigmoid(pre_gate)
    silu_gate = pre_gate * sigma
    hidden = (silu_gate * pre_up).astype(jnp.bfloat16)
    return (pre_gate, pre_up, sigma, silu_gate, hidden)


def spread(buffer, groups, capacity):
    width = buffer.shape[-1]
    blocks = buffer.reshape(groups, capacity, width)
    arrived = lax.all_to_all(blocks, "expert", split_axis=0, concat_axis=0, tiled=True)
    return arrived.reshape(-1, width)


def return_rows(term_fn, rows, groups, capacity, width):
    shares = lax.psum_scatter(
        term_fn(jnp.int32(0), rows * lax.axis_size("fsdp")).astype(jnp.bfloat16),
        "fsdp",
        scatter_dimension=0,
        tiled=True,
    )
    summed = lax.all_gather(shares, "fsdp", axis=0, tiled=True)
    back = lax.all_to_all(
        summed.reshape(groups, capacity, width), "expert", split_axis=0, concat_axis=0, tiled=True
    )
    return back.reshape(-1, width)


def per_device(tokens, assignment, route_weight, cotangent, w_gate, w_up, w_down):
    tok_dev = tokens.shape[0]
    width = tokens.shape[1]
    groups = lax.axis_size("expert")
    capacity = max(2, 3 * tok_dev // groups)
    slot_count = groups * capacity
    share_rows = slot_count // lax.axis_size("fsdp")
    table = slot_table(assignment, groups, capacity)
    slot_ids = jnp.arange(slot_count, dtype=jnp.int32)
    pick_first = slot_ids[:, None] == table[:, 0][None, :]
    pick_second = slot_ids[:, None] == table[:, 1][None, :]
    pick_both = jnp.logical_or(pick_first, pick_second).astype(jnp.bfloat16)
    sent_tokens = jnp.dot(pick_both, tokens, preferred_element_type=jnp.float32).astype(
        jnp.bfloat16
    )
    weighted = (route_weight[:, :, None] * cotangent[:, None, :].astype(jnp.float32)).astype(
        jnp.bfloat16
    )
    sent_cot = (
        jnp.dot(pick_first.astype(jnp.bfloat16), weighted[:, 0], preferred_element_type=jnp.float32)
        + jnp.dot(
            pick_second.astype(jnp.bfloat16), weighted[:, 1], preferred_element_type=jnp.float32
        )
    ).astype(jnp.bfloat16)
    gate_local = w_gate[0]
    up_local = w_up[0]
    down_local = w_down[0]
    gathered = spread(sent_tokens, groups, capacity)
    pre_gate, pre_up, sigma, silu_gate, hidden = front_half(gathered, gate_local, up_local)

    def out_term(start, count):
        return jnp.dot(hidden, down_local, preferred_element_type=jnp.float32)

    out_back = return_rows(out_term, share_rows, groups, capacity, width).astype(jnp.float32)
    select_first = pick_first.astype(jnp.float32)
    select_second = pick_second.astype(jnp.float32)
    first_out = jnp.dot(select_first.T, out_back, precision=lax.Precision.HIGHEST)
    second_out = jnp.dot(select_second.T, out_back, precision=lax.Precision.HIGHEST)
    moe_out = (route_weight[:, 0:1] * first_out + route_weight[:, 1:2] * second_out).astype(
        jnp.bfloat16
    )
    cot_float = cotangent.astype(jnp.float32)
    grad_prob = jnp.stack(
        [jnp.sum(cot_float * first_out, axis=1), jnp.sum(cot_float * second_out, axis=1)], axis=1
    )
    grad_gathered = spread(sent_cot, groups, capacity)
    grad_hidden = jnp.dot(grad_gathered, down_local.T, preferred_element_type=jnp.float32)
    grad_down = jnp.dot(hidden.T, grad_gathered, preferred_element_type=jnp.float32).astype(
        jnp.bfloat16
    )
    grad_pre_gate = (grad_hidden * pre_up * sigma * (1.0 + pre_gate * (1.0 - sigma))).astype(
        jnp.bfloat16
    )
    grad_pre_up = (grad_hidden * silu_gate).astype(jnp.bfloat16)
    grad_gate = jnp.dot(gathered.T, grad_pre_gate, preferred_element_type=jnp.float32).astype(
        jnp.bfloat16
    )
    grad_up = jnp.dot(gathered.T, grad_pre_up, preferred_element_type=jnp.float32).astype(
        jnp.bfloat16
    )

    def back_term(start, count):
        return jnp.dot(grad_pre_gate, gate_local.T, preferred_element_type=jnp.float32) + jnp.dot(
            grad_pre_up, up_local.T, preferred_element_type=jnp.float32
        )

    grad_back = return_rows(back_term, share_rows, groups, capacity, width).astype(jnp.float32)
    grad_tokens = (
        jnp.dot(select_first.T, grad_back, precision=lax.Precision.HIGHEST)
        + jnp.dot(select_second.T, grad_back, precision=lax.Precision.HIGHEST)
    ).astype(jnp.bfloat16)
    return (moe_out, grad_tokens, grad_prob, grad_gate[None], grad_up[None], grad_down[None])


def solution(mesh):
    return jax.shard_map(
        per_device,
        mesh=mesh,
        in_specs=(
            P("expert", None),
            P("expert", None),
            P("expert", None),
            P("expert", None),
            P("expert", None, "fsdp"),
            P("expert", None, "fsdp"),
            P("expert", "fsdp", None),
        ),
        out_specs=(
            P("expert", None),
            P("expert", None),
            P("expert", None),
            P("expert", None, "fsdp"),
            P("expert", None, "fsdp"),
            P("expert", "fsdp", None),
        ),
        check_vma=False,
    )
```

profile of v0, /device:TPU:1, one launch (start us, length us, event | category | flops | bytes accessed | tf_op | source)
XLA Modules:
  0.0 461.6 jit_solution(11138213794973551333)
XLA Ops:
  13.6 6.0 %all-to-all-start = ((bf16[8,48,3072]{2,1,0:T(8,128)(2,1)}), bf16[8,48,3072]{2,1,0:T(8,128)(2,1)}, u32[]{:S(2)}, u32[]{:S(2)}) async-start(bf16[8,48,3072]{2,1,0:T(8,128)(2,1)} %bitcast.80), calls=%async_computation | async-start | bytes 4718592 | tf_op jit(solution)/shard_map/all_to_all | solution.py:27
  23.0 26.6 %all-to-all-done = bf16[8,48,3072]{2,1,0:T(8,128)(2,1)} async-done(((bf16[8,48,3072]{2,1,0:T(8,128)(2,1)}), bf16[8,48,3072]{2,1,0:T(8,128)(2,1)}, u32[]{:S(2)}, u32[]{:S(2)}) %all-to-all-start) | async-done | bytes 2359328 | tf_op jit(solution)/shard_map/all_to_all | solution.py:27
  49.6 4.4 all-to-all-start.2
  61.0 22.9 %all-to-all-done.2 = bf16[8,48,3072]{2,1,0:T(8,128)(2,1)} async-done(((bf16[8,48,3072]{2,1,0:T(8,128)(2,1)}), bf16[8,48,3072]{2,1,0:T(8,128)(2,1)}, u32[]{:S(2)}, u32[]{:S(2)}) %all-to-all-start.2) | async-done | bytes 2359328 | tf_op jit(solution)/shard_map/all_to_all | solution.py:27
  92.0 83.1 %fusion.34 = (bf16[16,3072]{1,0:T(8,128)(2,1)S(1)}, bf16[16,3072]{1,0:T(8,128)(2,1)S(1)}) fusion(bf16[384,3072]{1,0:T(8,128)(2,1)} %convolution_convert_fusion.1, bf16[384,3072]{1,0:T(8,128)(2,1)} %add_convert_fusion), kind=kCustom, calls=%all-reduce-scatter.2 | all-reduce-scatter fusion | flops 3145729 | bytes 4916224
  180.6 8.8 %collective-permute-start.2 = (bf16[16,3072]{1,0:T(8,128)(2,1)S(1)}, bf16[16,3072]{1,0:T(8,128)(2,1)S(1)}, u32[]{:S(2)}, u32[]{:S(2)}) collective-permute-start(bf16[16,3072]{1,0:T(8,128)(2,1)S(1)} %get-tuple-element.10), channel_id=1, source_target_pairs={{0,3},{1,4},{2,5},{3,6},{4,7},{5,8},{6,9},{7,10},{8,11},{9,12},{10... | collective-permute-start | bytes 294920
  189.4 6.9 %collective-permute-start.3 = (bf16[16,3072]{1,0:T(8,128)(2,1)S(1)}, bf16[16,3072]{1,0:T(8,128)(2,1)S(1)}, u32[]{:S(2)}, u32[]{:S(2)}) collective-permute-start(bf16[16,3072]{1,0:T(8,128)(2,1)S(1)} %get-tuple-element.10), channel_id=1, source_target_pairs={{0,4},{1,5},{2,6},{3,7},{4,8},{5,9},{6,10},{7,11},{8,12},{9,13},{1... | collective-permute-start | bytes 294920
  200.5 7.4 %collective-permute-start.6 = (bf16[16,3072]{1,0:T(8,128)(2,1)S(1)}, bf16[16,3072]{1,0:T(8,128)(2,1)}, u32[]{:S(2)}, u32[]{:S(2)}) collective-permute-start(bf16[16,3072]{1,0:T(8,128)(2,1)S(1)} %get-tuple-element.10), channel_id=1, source_target_pairs={{0,7},{1,8},{2,9},{3,10},{4,11},{5,12},{6,13},{7,14},{8,15},{9,16}... | collective-permute-start | bytes 294920
  212.4 4.5 collective-permute-done.6
  216.8 6.5 %concatenate = bf16[140,3072]{1,0:T(8,128)(2,1)S(1)} concatenate(bf16[12,3072]{1,0:T(8,128)(2,1)S(1)} %collective-permute-done.7, bf16[16,3072]{1,0:T(8,128)(2,1)} %collective-permute-done.6, bf16[16,3072]{1,0:T(8,128)(2,1)} %copy-done.8, bf16[16,3072]{1,0:T(8,128)(2,1)} %copy-done.7, bf16[16,3072]{1,0:T(8,128)(2,1)S(1)} %collective-permute-done.3, ...), dimensions={0} | concatenate | bytes 1720320
  225.7 9.2 %collective-permute-start.11 = (bf16[16,3072]{1,0:T(8,128)(2,1)S(1)}, bf16[16,3072]{1,0:T(8,128)(2,1)S(1)}, u32[]{:S(2)}, u32[]{:S(2)}) collective-permute-start(bf16[16,3072]{1,0:T(8,128)(2,1)S(1)} %get-tuple-element.11), channel_id=1, source_target_pairs={{0,4},{1,5},{2,6},{3,7},{4,8},{5,9},{6,10},{7,11},{8,12},{9,13},{1... | collective-permute-start | bytes 294920
  234.9 7.5 %collective-permute-start.15 = (bf16[12,3072]{1,0:T(8,128)(2,1)S(1)}, bf16[12,3072]{1,0:T(8,128)(2,1)S(1)}, u32[]{:S(2)}, u32[]{:S(2)}) collective-permute-start(bf16[12,3072]{1,0:T(8,128)(2,1)S(1)} %slice.36), channel_id=1, source_target_pairs={{0,8},{1,9},{2,10},{3,11},{4,12},{5,13},{6,14},{7,15},{8,16},{9,17... | collective-permute-start | bytes 221192
  248.5 6.2 %collective-permute-start.8 = (bf16[16,3072]{1,0:T(8,128)(2,1)S(1)}, bf16[16,3072]{1,0:T(8,128)(2,1)S(1)}, u32[]{:S(2)}, u32[]{:S(2)}) collective-permute-start(bf16[16,3072]{1,0:T(8,128)(2,1)S(1)} %get-tuple-element.11), channel_id=1, source_target_pairs={{0,1},{1,2},{2,3},{3,4},{4,5},{5,6},{6,7},{7,8},{8,9},{9,10},{10,1... | collective-permute-start | bytes 294920
  256.7 4.3 collective-permute-done.14
  267.4 5.1 %concatenate.1 = bf16[140,3072]{1,0:T(8,128)(2,1)S(1)} concatenate(bf16[12,3072]{1,0:T(8,128)(2,1)S(1)} %collective-permute-done.15, bf16[16,3072]{1,0:T(8,128)(2,1)S(1)} %collective-permute-done.14, bf16[16,3072]{1,0:T(8,128)(2,1)S(1)} %collective-permute-done.13, bf16[16,3072]{1,0:T(8,128)(2,1)S(1)} %collective-permute-done.12, bf16[16,3072]{1,0:T(8,128)(2,1)S(1)} %collective-permute-done.11, ...), dimensions={0} | concatenate | bytes 1720320
  273.2 37.1 %all-gather.5.cloned.1.call-done = bf16[32,12,3072]{2,1,0:T(8,128)(2,1)} async-done(((bf16[1,12,3072]{2,1,0:T(8,128)(2,1)}), bf16[32,12,3072]{2,1,0:T(8,128)(2,1)}) %all-gather.5.cloned.1.call-update) | async-done | bytes 2359312 | tf_op jit(solution)/shard_map/all_gather | solution.py:38
  310.3 4.3 reshape.64
  314.6 4.4 all-to-all-start.1
  319.0 87.6 %all-gather.7.cloned.1.call-done = bf16[32,12,3072]{2,1,0:T(8,128)(2,1)} async-done(((bf16[1,12,3072]{2,1,0:T(8,128)(2,1)}), bf16[32,12,3072]{2,1,0:T(8,128)(2,1)}) %all-gather.7.cloned.1.call-update) | async-done | bytes 2359312 | tf_op jit(solution)/shard_map/all_gather | solution.py:38
  406.6 4.2 reshape.68
  410.8 4.6 all-to-all-start.3
  419.7 3.9 fusion.2
  423.6 3.8 fusion.3
  429.7 15.4 %all-to-all-done.3 = bf16[8,48,3072]{2,1,0:T(8,128)(2,1)} async-done(((bf16[8,48,3072]{2,1,0:T(8,128)(2,1)}), bf16[8,48,3072]{2,1,0:T(8,128)(2,1)}, u32[]{:S(2)}, u32[]{:S(2)}) %all-to-all-start.3) | async-done | bytes 2359328 | tf_op jit(solution)/shard_map/all_to_all | solution.py:39
  (91 shorter events, 71.9 us)
Async XLA Ops:
  7.2 76.7 %copy-start = (bf16[1,256,3072]{2,1,0:T(8,128)(2,1)S(1)}, bf16[1,256,3072]{2,1,0:T(8,128)(2,1)}, u32[]{:S(2)}) copy-start(bf16[1,256,3072]{2,1,0:T(8,128)(2,1)} %param.13) | copy-start | bytes 4718596
  13.6 36.0 %all-to-all-start = ((bf16[8,48,3072]{2,1,0:T(8,128)(2,1)}), bf16[8,48,3072]{2,1,0:T(8,128)(2,1)}, u32[]{:S(2)}, u32[]{:S(2)}) async-start(bf16[8,48,3072]{2,1,0:T(8,128)(2,1)} %bitcast.80), calls=%async_computation | async-start | bytes 4718592 | tf_op jit(solution)/shard_map/all_to_all | solution.py:27
  49.6 34.3 %all-to-all-start.2 = ((bf16[8,48,3072]{2,1,0:T(8,128)(2,1)}), bf16[8,48,3072]{2,1,0:T(8,128)(2,1)}, u32[]{:S(2)}, u32[]{:S(2)}) async-start(bf16[8,48,3072]{2,1,0:T(8,128)(2,1)} %bitcast.81), calls=%async_computation.2 | async-start | bytes 4718592 | tf_op jit(solution)/shard_map/all_to_all | solution.py:27
  54.0 256.3 %all-gather.5.cloned.1.call-start = ((), (), s32[]{:S(2)}) async-start(), calls=%async_computation.4 | async-start | bytes 3244032 | tf_op jit(solution)/shard_map/all_gather | solution.py:38
  92.0 115.9 %copy-start.12 = (u32[256]{0:T(256)S(1)}, u32[256]{0:T(256)}, u32[]{:S(2)}) copy-start(u32[256]{0:T(256)} %constant.17) | copy-start | bytes 3076
  175.1 24.1 %collective-permute-start = (bf16[16,3072]{1,0:T(8,128)(2,1)S(1)}, bf16[16,3072]{1,0:T(8,128)(2,1)S(1)}, u32[]{:S(2)}, u32[]{:S(2)}) collective-permute-start(bf16[16,3072]{1,0:T(8,128)(2,1)S(1)} %get-tuple-element.10), channel_id=1, source_target_pairs={{0,1},{1,2},{2,3},{3,4},{4,5},{5,6},{6,7},{7,8},{8,9},{9,10},{10,1... | collective-permute-start | bytes 294920
  177.9 22.6 %collective-permute-start.1 = (bf16[16,3072]{1,0:T(8,128)(2,1)S(1)}, bf16[16,3072]{1,0:T(8,128)(2,1)S(1)}, u32[]{:S(2)}, u32[]{:S(2)}) collective-permute-start(bf16[16,3072]{1,0:T(8,128)(2,1)S(1)} %get-tuple-element.10), channel_id=1, source_target_pairs={{0,2},{1,3},{2,4},{3,5},{4,6},{5,7},{6,8},{7,9},{8,10},{9,11},{10,... | collective-permute-start | bytes 294920
  179.3 17.1 %collective-permute-start.7 = (bf16[12,3072]{1,0:T(8,128)(2,1)S(1)}, bf16[12,3072]{1,0:T(8,128)(2,1)S(1)}, u32[]{:S(2)}, u32[]{:S(2)}) collective-permute-start(bf16[12,3072]{1,0:T(8,128)(2,1)S(1)} %slice.35), channel_id=1, source_target_pairs={{0,8},{1,9},{2,10},{3,11},{4,12},{5,13},{6,14},{7,15},{8,16},{9,17... | collective-permute-start | bytes 221192
  180.6 28.6 %collective-permute-start.2 = (bf16[16,3072]{1,0:T(8,128)(2,1)S(1)}, bf16[16,3072]{1,0:T(8,128)(2,1)S(1)}, u32[]{:S(2)}, u32[]{:S(2)}) collective-permute-start(bf16[16,3072]{1,0:T(8,128)(2,1)S(1)} %get-tuple-element.10), channel_id=1, source_target_pairs={{0,3},{1,4},{2,5},{3,6},{4,7},{5,8},{6,9},{7,10},{8,11},{9,12},{10... | collective-permute-start | bytes 294920
  189.4 19.7 %collective-permute-start.3 = (bf16[16,3072]{1,0:T(8,128)(2,1)S(1)}, bf16[16,3072]{1,0:T(8,128)(2,1)S(1)}, u32[]{:S(2)}, u32[]{:S(2)}) collective-permute-start(bf16[16,3072]{1,0:T(8,128)(2,1)S(1)} %get-tuple-element.10), channel_id=1, source_target_pairs={{0,4},{1,5},{2,6},{3,7},{4,8},{5,9},{6,10},{7,11},{8,12},{9,13},{1... | collective-permute-start | bytes 294920
  196.4 12.8 %collective-permute-start.4 = (bf16[16,3072]{1,0:T(8,128)(2,1)S(1)}, bf16[16,3072]{1,0:T(8,128)(2,1)S(1)}, u32[]{:S(2)}, u32[]{:S(2)}) collective-permute-start(bf16[16,3072]{1,0:T(8,128)(2,1)S(1)} %get-tuple-element.10), channel_id=1, source_target_pairs={{0,5},{1,6},{2,7},{3,8},{4,9},{5,10},{6,11},{7,12},{8,13},{9,14},{... | collective-permute-start | bytes 294920
  199.1 12.6 %collective-permute-start.5 = (bf16[16,3072]{1,0:T(8,128)(2,1)S(1)}, bf16[16,3072]{1,0:T(8,128)(2,1)S(1)}, u32[]{:S(2)}, u32[]{:S(2)}) collective-permute-start(bf16[16,3072]{1,0:T(8,128)(2,1)S(1)} %get-tuple-element.10), channel_id=1, source_target_pairs={{0,6},{1,7},{2,8},{3,9},{4,10},{5,11},{6,12},{7,13},{8,14},{9,15},... | collective-permute-start | bytes 294920
  200.5 16.3 %collective-permute-start.6 = (bf16[16,3072]{1,0:T(8,128)(2,1)S(1)}, bf16[16,3072]{1,0:T(8,128)(2,1)}, u32[]{:S(2)}, u32[]{:S(2)}) collective-permute-start(bf16[16,3072]{1,0:T(8,128)(2,1)S(1)} %get-tuple-element.10), channel_id=1, source_target_pairs={{0,7},{1,8},{2,9},{3,10},{4,11},{5,12},{6,13},{7,14},{8,15},{9,16}... | collective-permute-start | bytes 294920
  224.1 182.5 %all-gather.7.cloned.1.call-start = ((), (), s32[]{:S(2)}) async-start(), calls=%async_computation.5 | async-start | bytes 3244032 | tf_op jit(solution)/shard_map/all_gather | solution.py:38
  224.1 24.4 %collective-permute-start.10 = (bf16[16,3072]{1,0:T(8,128)(2,1)S(1)}, bf16[16,3072]{1,0:T(8,128)(2,1)S(1)}, u32[]{:S(2)}, u32[]{:S(2)}) collective-permute-start(bf16[16,3072]{1,0:T(8,128)(2,1)S(1)} %get-tuple-element.11), channel_id=1, source_target_pairs={{0,3},{1,4},{2,5},{3,6},{4,7},{5,8},{6,9},{7,10},{8,11},{9,12},{10... | collective-permute-start | bytes 294920
  225.7 29.1 %collective-permute-start.11 = (bf16[16,3072]{1,0:T(8,128)(2,1)S(1)}, bf16[16,3072]{1,0:T(8,128)(2,1)S(1)}, u32[]{:S(2)}, u32[]{:S(2)}) collective-permute-start(bf16[16,3072]{1,0:T(8,128)(2,1)S(1)} %get-tuple-element.11), channel_id=1, source_target_pairs={{0,4},{1,5},{2,6},{3,7},{4,8},{5,9},{6,10},{7,11},{8,12},{9,13},{1... | collective-permute-start | bytes 294920
  234.9 11.7 %collective-permute-start.15 = (bf16[12,3072]{1,0:T(8,128)(2,1)S(1)}, bf16[12,3072]{1,0:T(8,128)(2,1)S(1)}, u32[]{:S(2)}, u32[]{:S(2)}) collective-permute-start(bf16[12,3072]{1,0:T(8,128)(2,1)S(1)} %slice.36), channel_id=1, source_target_pairs={{0,8},{1,9},{2,10},{3,11},{4,12},{5,13},{6,14},{7,15},{8,16},{9,17... | collective-permute-start | bytes 221192
  242.5 14.2 %collective-permute-start.12 = (bf16[16,3072]{1,0:T(8,128)(2,1)S(1)}, bf16[16,3072]{1,0:T(8,128)(2,1)S(1)}, u32[]{:S(2)}, u32[]{:S(2)}) collective-permute-start(bf16[16,3072]{1,0:T(8,128)(2,1)S(1)} %get-tuple-element.11), channel_id=1, source_target_pairs={{0,5},{1,6},{2,7},{3,8},{4,9},{5,10},{6,11},{7,12},{8,13},{9,14},{... | collective-permute-start | bytes 294920
  243.8 12.9 %collective-permute-start.13 = (bf16[16,3072]{1,0:T(8,128)(2,1)S(1)}, bf16[16,3072]{1,0:T(8,128)(2,1)S(1)}, u32[]{:S(2)}, u32[]{:S(2)}) collective-permute-start(bf16[16,3072]{1,0:T(8,128)(2,1)S(1)} %get-tuple-element.11), channel_id=1, source_target_pairs={{0,6},{1,7},{2,8},{3,9},{4,10},{5,11},{6,12},{7,13},{8,14},{9,15},... | collective-permute-start | bytes 294920
  246.6 14.4 %collective-permute-start.14 = (bf16[16,3072]{1,0:T(8,128)(2,1)S(1)}, bf16[16,3072]{1,0:T(8,128)(2,1)S(1)}, u32[]{:S(2)}, u32[]{:S(2)}) collective-permute-start(bf16[16,3072]{1,0:T(8,128)(2,1)S(1)} %get-tuple-element.11), channel_id=1, source_target_pairs={{0,7},{1,8},{2,9},{3,10},{4,11},{5,12},{6,13},{7,14},{8,15},{9,16}... | collective-permute-start | bytes 294920
  248.5 16.1 %collective-permute-start.8 = (bf16[16,3072]{1,0:T(8,128)(2,1)S(1)}, bf16[16,3072]{1,0:T(8,128)(2,1)S(1)}, u32[]{:S(2)}, u32[]{:S(2)}) collective-permute-start(bf16[16,3072]{1,0:T(8,128)(2,1)S(1)} %get-tuple-element.11), channel_id=1, source_target_pairs={{0,1},{1,2},{2,3},{3,4},{4,5},{5,6},{6,7},{7,8},{8,9},{9,10},{10,1... | collective-permute-start | bytes 294920
  254.8 12.7 %collective-permute-start.9 = (bf16[16,3072]{1,0:T(8,128)(2,1)S(1)}, bf16[16,3072]{1,0:T(8,128)(2,1)}, u32[]{:S(2)}, u32[]{:S(2)}) collective-permute-start(bf16[16,3072]{1,0:T(8,128)(2,1)S(1)} %get-tuple-element.11), channel_id=1, source_target_pairs={{0,2},{1,3},{2,4},{3,5},{4,6},{5,7},{6,8},{7,9},{8,10},{9,11},{10,... | collective-permute-start | bytes 294920
  314.6 96.2 %all-to-all-start.1 = ((bf16[8,48,3072]{2,1,0:T(8,128)(2,1)}), bf16[8,48,3072]{2,1,0:T(8,128)(2,1)}, u32[]{:S(2)}, u32[]{:S(2)}) async-start(bf16[8,48,3072]{2,1,0:T(8,128)(2,1)} %reshape.64), calls=%async_computation.1 | async-start | bytes 4718592 | tf_op jit(solution)/shard_map/all_to_all | solution.py:39
  410.8 34.3 %all-to-all-start.3 = ((bf16[8,48,3072]{2,1,0:T(8,128)(2,1)}), bf16[8,48,3072]{2,1,0:T(8,128)(2,1)}, u32[]{:S(2)}, u32[]{:S(2)}) async-start(bf16[8,48,3072]{2,1,0:T(8,128)(2,1)} %reshape.68), calls=%async_computation.3 | async-start | bytes 4718592 | tf_op jit(solution)/shard_map/all_to_all | solution.py:39
  (11 other events, 35.5 us)
Sparse Core Ops, SparseCore 0:
  224.2 86.0 all-gather.4
  313.7 92.8 all-gather.6
where the time goes:
time: 468 us; the launch traced here: 462 us
  waiting for transfers between devices  207 us (44%)
  starting transfers between devices  84.5 us (18%)
  blocking collectives  83.1 us (18%)
  matrix products  44.1 us (9%)
  local copies, waits for them, and re-layouts  25.5 us (5%)
  between operations  15.1 us (3%)
    all_gather x2, waiting for transfers between devices, return_rows(): summed = lax.all_gather(shares, 'fsdp', axis=0, tiled=True)  125 us
    unnamed x1, blocking collectives  83.1 us
    unnamed x16, starting transfers between devices  65.1 us
    all_to_all x2, waiting for transfers between devices, spread(): lax.all_to_all(blocks, 'expert', split_axis=0, concat_axis=0, tiled=True)  49.5 us
    unnamed x18, waiting for transfers between devices  17.2 us
    unnamed x34, local copies, waits for them, and re-layouts  15.8 us
    all_to_all x2, waiting for transfers between devices, return_rows(): lax.all_to_all(summed.reshape(groups, capacity, width), 'expert', split_a...  15.4 us
    all_to_all x2, starting transfers between devices, spread(): lax.all_to_all(blocks, 'expert', split_axis=0, concat_axis=0, tiled=True)  10.4 us
  transfers between devices with their start and end apart: 22, of which 10 were waited for; matrix products, arithmetic and copies ran while one was open for 9% of the time, Pallas kernels for 0%

commit v1 on v0

v1 whole, which is shorter than its diff:
```python
import functools

import jax
import jax.numpy as jnp
from jax import lax
from jax.experimental import pallas as pl
from jax.experimental.pallas import tpu as pltpu
from jax.sharding import PartitionSpec as P

MESH = pl.DeviceIdType.MESH
BF16 = jnp.bfloat16
F32 = jnp.float32
NT = (((1,), (1,)), ((), ()))
TN = (((0,), (0,)), ((), ()))

E = 8
NZ = 8
CAP = 48
TOK = 128
SLOTS = E * CAP
D = 3072
H = 256
HALF = SLOTS // 2
KS = 256
NK = D // KS
ND = NK - NZ
RS = D // NZ


def rows_of(index, size):
    return pl.ds(pl.multiple_of(index * size, size), size)


def kernel(
    tokens, assignment, weight, cotangent, w_gate, w_up, w_down,
    moe_out, grad_tokens, grad_prob, grad_gate, grad_up, grad_down,
    acts, cot_part, wgu, wd, send_s, send_d, xd, acc_gu, acc_h, hid, gpre,
    part, rp, rm, rc, gp, outs, gg, gu, gd,
    load_sem, wpre_sem, store_sem,
    a_send, a_recv, d_send, d_recv, ring_send, ring_recv, sib_send, sib_recv, dsib_sem,
    act_sem, rs_send, rs_recv, c_send, c_recv, o_send, o_recv, osib_send, osib_recv, g_send, g_recv,
):
    e = lax.axis_index("expert")
    f = lax.axis_index("fsdp")
    core = lax.rem(f, 2)
    z = lax.rem(lax.div(f, 2), NZ)
    yh = lax.div(f, 2 * NZ)
    t = core

    def dev(e_, yh_, z_, c_):
        return (e_, yh_ * (2 * NZ) + z_ * 2 + c_)

    sibling = dev(e, yh, z, 1 - core)
    up = dev(e, yh, lax.rem(z + 1, NZ), core)
    down = dev(e, yh, lax.rem(z + NZ - 1, NZ), core)

    def zmod(v):
        return lax.rem(v + 2 * NZ, NZ)

    pending = []

    def remote(src, dst, ss, rs, device):
        return pltpu.make_async_remote_copy(
            src_ref=src, dst_ref=dst, send_sem=ss, recv_sem=rs, device_id=device, device_id_type=MESH
        )

    def send(src, dst, ss, rs, device):
        c = remote(src, dst, ss, rs, device)
        c.start()
        pending.append(c)

    def arrived(dst, ss, rs):
        remote(dst, dst, ss, rs, sibling).wait_recv()

    load_x = pltpu.make_async_copy(tokens, acts, load_sem.at[0])
    load_y = pltpu.make_async_copy(cotangent, acts, load_sem.at[0])

    @pl.when(core == 0)
    def _():
        load_x.start()

    @pl.when(core == 1)
    def _():
        load_y.start()

    own_g = pltpu.make_async_copy(w_gate.at[0], wgu.at[:, rows_of(core, H)], load_sem.at[1])
    own_u = pltpu.make_async_copy(w_up.at[0], wgu.at[:, rows_of(core + 2, H)], load_sem.at[2])
    own_d = pltpu.make_async_copy(w_down.at[0], wd.at[rows_of(core, H), :], load_sem.at[3])
    own_c = pltpu.make_async_copy(cotangent.at[:, rows_of(z, RS)], cot_part, load_sem.at[4])
    for c in (own_g, own_u, own_d, own_c):
        c.start()

    barrier = pltpu.get_barrier_semaphore()

    def greet(device):
        pl.semaphore_signal(barrier, inc=1, device_id=device, device_id_type=MESH)

    for i in range(E):
        for dy in range(2):
            if i or dy:
                greet(dev(lax.rem(e + i, E), lax.rem(yh + dy, 2), z, core))
    for dz in range(NZ):
        for dc in range(2):
            if dz or dc:
                greet(dev(e, yh, lax.rem(z + dz, NZ), lax.rem(core + dc, 2)))

    a = assignment[...]
    rw = weight[...]
    lane = lax.broadcasted_iota(jnp.int32, (TOK, TOK), 1)
    row = lax.broadcasted_iota(jnp.int32, (TOK, TOK), 0)
    hot0 = (a[:, 0:1] == lane).astype(F32)
    hot1 = (a[:, 1:2] == lane).astype(F32)
    below = (row > lane).astype(BF16)
    count = jnp.dot(below, (hot0 + hot1).astype(BF16), preferred_element_type=F32)
    pos0 = jnp.sum(hot0 * count, axis=1, keepdims=True)
    pos1 = jnp.sum(hot1 * count, axis=1, keepdims=True)
    slot0 = a[:, 0:1] * CAP + pos0.astype(jnp.int32)
    slot1 = a[:, 1:2] * CAP + pos1.astype(jnp.int32)
    slot_lane = lax.broadcasted_iota(jnp.int32, (TOK, SLOTS), 1)
    pick0 = (slot0 == slot_lane).astype(F32)
    pick1 = (slot1 == slot_lane).astype(F32)
    spread = jnp.concatenate([pick0.T, pick1.T], axis=1).astype(BF16)
    w0 = rw[:, 0:1]
    w1 = rw[:, 1:2]
    is_x = core == 0
    in0 = jnp.where(is_x, 1.0, w0)
    in1 = jnp.where(is_x, 1.0, w1)

    def dispatch(cols):
        v = cols.astype(F32)
        both = jnp.concatenate([(in0 * v).astype(BF16), (in1 * v).astype(BF16)], axis=0)
        return jnp.dot(spread, both, preferred_element_type=F32).astype(BF16)

    @pl.when(core == 0)
    def _():
        load_x.wait()

    @pl.when(core == 1)
    def _():
        load_y.wait()

    send_s[...] = dispatch(acts[:, rows_of(z, KS)])
    own_rows = rows_of(e, CAP)
    xd[t, z, own_rows, :] = send_s[own_rows, :]

    pl.semaphore_wait(barrier, 2 * E - 1 + 2 * NZ - 1)

    for i in range(1, E):
        j = lax.rem(e + i, E)
        send(
            send_s.at[rows_of(j, CAP), :], xd.at[t, z, own_rows, :],
            a_send.at[i - 1], a_recv.at[i - 1], dev(j, yh, z, core),
        )

    @pl.when(core == 0)
    def _():
        remote(w_gate.at[0], wgu.at[:, 0:H], wpre_sem.at[0], wpre_sem.at[2], sibling).start()
        remote(w_up.at[0], wgu.at[:, 2 * H : 3 * H], wpre_sem.at[1], wpre_sem.at[3], sibling).start()

    @pl.when(core == 1)
    def _():
        remote(w_down.at[0], wd.at[H : 2 * H, :], wpre_sem.at[0], wpre_sem.at[2], sibling).start()

    for k in range(ND):
        send_d[k] = dispatch(acts[:, (NZ + k) * KS : (NZ + k + 1) * KS])
    for k in range(ND):
        xd[t, NZ + k, own_rows, :] = send_d[k, own_rows, :]
    for i in range(1, E):
        j = lax.rem(e + i, E)
        send(
            send_d.at[:, rows_of(j, CAP), :], xd.at[t, NZ:NK, own_rows, :],
            d_send.at[i - 1], d_recv.at[i - 1], dev(j, yh, z, core),
        )

    def gather(view, sems, slot, after_step):
        s_send, s_recv, b_send, b_recv = sems

        def pass_on(d, h):
            ref = view(slot, zmod(z + d), h)
            send(ref, ref, b_send.at[d % NZ, h], b_recv.at[d % NZ, h], sibling)

        for s in range(5):
            for h in range(2):
                for way, nxt, sign in ((0, up, -1), (1, down, 1)):
                    full = s < 4 or h == way
                    if not full:
                        continue
                    ref = view(slot, zmod(z + sign * s), h)
                    if s > 0:
                        arrived(ref, s_send.at[way, s - 1, h], s_recv.at[way, s - 1, h])
                    if s < 3 or (s == 3 and h == way):
                        send(ref, ref, s_send.at[way, s, h], s_recv.at[way, s, h], nxt)
                    if s > 0 or way == 0:
                        pass_on(sign * s, h)
            after_step(s)

    def xd_view(slot, zz, h):
        return xd.at[slot, zz, h * HALF : (h + 1) * HALF, :]

    for i in range(1, E):
        src = rows_of(lax.rem(e + E - i, E), CAP)
        arrived(xd.at[t, z, src, :], a_send.at[i - 1], a_recv.at[i - 1])

    def nothing(s):
        pass

    gather(xd_view, (ring_send, ring_recv, sib_send, sib_recv), t, nothing)

    for i in range(1, E):
        src = rows_of(lax.rem(e + E - i, E), CAP)
        arrived(xd.at[t, NZ:NK, src, :], d_send.at[i - 1], d_recv.at[i - 1])
    send(xd.at[t, NZ:NK], xd.at[t, NZ:NK], dsib_sem.at[0], dsib_sem.at[1], sibling)
    other = 1 - t
    for d in range(NZ):
        for h in range(2):
            arrived(xd_view(other, zmod(z + d), h), sib_send.at[d, h], sib_recv.at[d, h])
    arrived(xd.at[other, NZ:NK], dsib_sem.at[0], dsib_sem.at[1])
    for c in (own_g, own_u, own_d, own_c):
        c.wait()

    mine_g = rows_of(core, H)
    mine_u = rows_of(core + 2, H)
    acc_gu[...] = jnp.zeros_like(acc_gu)
    acc_h[...] = jnp.zeros_like(acc_h)

    @pl.loop(0, NK)
    def _(k):
        kr = rows_of(k, KS)
        acc_gu[:, 0:H] += jnp.dot(xd[0, k], wgu[kr, mine_g], preferred_element_type=F32)
        acc_gu[:, H : 2 * H] += jnp.dot(xd[0, k], wgu[kr, mine_u], preferred_element_type=F32)
        acc_h[...] += lax.dot_general(xd[1, k], wd[mine_g, kr], NT, preferred_element_type=F32)

    @pl.loop(0, E)
    def _(b):
        r = rows_of(b, CAP)
        pre_gate = acc_gu[r, 0:H]
        pre_up = acc_gu[r, H : 2 * H]
        grad_hidden = acc_h[r, :]
        sigma = jax.nn.sigmoid(pre_gate)
        silu = pre_gate * sigma
        hid[r, mine_g] = (silu * pre_up).astype(BF16)
        gpre[r, mine_g] = (grad_hidden * pre_up * sigma * (1.0 + pre_gate * (1.0 - sigma))).astype(BF16)
        gpre[r, mine_u] = (grad_hidden * silu).astype(BF16)

    @pl.when(core == 0)
    def _():
        cg = remote(gpre.at[:, 0:H], gpre.at[:, 0:H], act_sem.at[0], act_sem.at[2], sibling)
        cu = remote(gpre.at[:, 2 * H : 3 * H], gpre.at[:, 2 * H : 3 * H], act_sem.at[1], act_sem.at[3], sibling)
        cg.start()
        cu.start()
        arrived(wd.at[H : 2 * H, :], wpre_sem.at[0], wpre_sem.at[2])
        arrived(hid.at[:, H : 2 * H], act_sem.at[0], act_sem.at[2])

    @pl.when(core == 1)
    def _():
        ch = remote(hid.at[:, H : 2 * H], hid.at[:, H : 2 * H], act_sem.at[0], act_sem.at[2], sibling)
        ch.start()
        arrived(wgu.at[:, 0:H], wpre_sem.at[0], wpre_sem.at[2])
        arrived(wgu.at[:, 2 * H : 3 * H], wpre_sem.at[1], wpre_sem.at[3])
        arrived(gpre.at[:, 0:H], act_sem.at[0], act_sem.at[2])
        arrived(gpre.at[:, 2 * H : 3 * H], act_sem.at[1], act_sem.at[3])

    def term(zd):
        cols = rows_of(zd, RS)

        @pl.when(core == 0)
        def _():
            part[zd] = jnp.dot(hid[...], wd[:, cols], preferred_element_type=F32).astype(BF16)

        @pl.when(core == 1)
        def _():
            part[zd] = lax.dot_general(gpre[...], wgu[cols, :], NT, preferred_element_type=F32).astype(BF16)

    land = (rp, rm)

    def half(h):
        return slice(h * HALF, (h + 1) * HALF)

    def target(way, s):
        return zmod(z + 4 - s) if way == 0 else zmod(z - 4 + s)

    def rs_start(way, s, h):
        send(
            part.at[target(way, s), half(h), :], land[way].at[s, half(h), :],
            rs_send.at[way, s, h], rs_recv.at[way, s, h], up if way == 0 else down,
        )

    def rs_arrived(way, s, h):
        arrived(land[way].at[s, half(h), :], rs_send.at[way, s, h], rs_recv.at[way, s, h])

    def rs_add(way, s, h):
        zd = target(way, s + 1)
        part[zd, half(h), :] = (
            part[zd, half(h), :].astype(F32) + land[way][s, half(h), :].astype(F32)
        ).astype(BF16)

    term(zmod(z + 4))
    rs_start(0, 0, 0)
    rs_start(1, 0, 1)
    term(zmod(z + 3))
    rs_start(0, 1, 1)
    term(zmod(z + 5))
    rs_start(1, 1, 0)

    @pl.loop(0, 5)
    def _(i):
        term(zmod(z + 6 + i))

    @pl.loop(0, NK)
    def _(k):
        kr = rows_of(k, KS)
        g = lax.dot_general(xd[0, k], gpre[:, mine_g], TN, preferred_element_type=F32)
        gg[kr, :] = g.astype(BF16)
        u = lax.dot_general(xd[0, k], gpre[:, mine_u], TN, preferred_element_type=F32)
        gu[kr, :] = u.astype(BF16)
        w = lax.dot_general(hid[:, mine_g], xd[1, k], TN, preferred_element_type=F32)
        gd[:, kr] = w.astype(BF16)

    store_g = pltpu.make_async_copy(gg, grad_gate.at[0], store_sem.at[0])
    store_u = pltpu.make_async_copy(gu, grad_up.at[0], store_sem.at[1])
    store_d = pltpu.make_async_copy(gd, grad_down.at[0], store_sem.at[2])
    for c in (store_g, store_u, store_d):
        c.start()

    for way, h in ((0, 0), (1, 1)):
        rs_arrived(way, 0, h)
        rs_add(way, 0, h)
        rs_start(way, 1, h)
    for s in (1, 2):
        for way, h in ((0, 1), (1, 0), (0, 0), (1, 1)):
            rs_arrived(way, s, h)
            rs_add(way, s, h)
            rs_start(way, s + 1, h)
    for h in range(2):
        for way in range(2):
            rs_arrived(way, 3, h)
        part[z, half(h), :] = (
            part[z, half(h), :].astype(F32)
            + rp[3, half(h), :].astype(F32)
            + rm[3, half(h), :].astype(F32)
        ).astype(BF16)

    rc[yh, own_rows, :] = part[z, own_rows, :]
    for i in range(E):
        for dy in range(2):
            if i or dy:
                b = lax.rem(e + i, E)
                send(
                    part.at[z, rows_of(b, CAP), :], rc.at[yh, own_rows, :],
                    c_send.at[i, dy], c_recv.at[i, dy], dev(b, lax.rem(yh + dy, 2), z, core),
                )
    for i in range(E):
        for dy in range(2):
            if i or dy:
                src = rows_of(lax.rem(e + E - i, E), CAP)
                arrived(rc.at[lax.rem(yh + dy, 2), src, :], c_send.at[i, dy], c_recv.at[i, dy])

    summed = (rc[0].astype(F32) + rc[1].astype(F32)).astype(BF16)
    out0 = jnp.dot(pick0.astype(BF16), summed, preferred_element_type=F32)
    out1 = jnp.dot(pick1.astype(BF16), summed, preferred_element_type=F32)
    on0 = jnp.where(is_x, w0, 1.0)
    on1 = jnp.where(is_x, w1, 1.0)
    outs[t, z] = (on0 * out0 + on1 * out1).astype(BF16)
    cot = cot_part[...].astype(F32)
    p0 = jnp.sum(cot * out0, axis=1, keepdims=True)
    p1 = jnp.sum(cot * out1, axis=1, keepdims=True)
    both = jnp.where(lane == 0, p0, 0.0) + jnp.where(lane == 1, p1, 0.0)

    @pl.when(core == 0)
    def _():
        gp[z] = both.T[0:8, :]
        for dz in range(NZ):
            for dc in range(2):
                if dz or dc:
                    remote(
                        gp.at[z], gp.at[z], g_send.at[dz, dc], g_recv.at[dz, dc],
                        dev(e, yh, lax.rem(z + dz, NZ), dc),
                    ).start()

    def out_view(slot, zz, h):
        return outs.at[slot, zz, h * (TOK // 2) : (h + 1) * (TOK // 2), :]

    gather(out_view, (o_send, o_recv, osib_send, osib_recv), t, nothing)

    for d in range(NZ):
        for h in range(2):
            arrived(out_view(other, zmod(z + d), h), osib_send.at[d, h], osib_recv.at[d, h])
    for zz in range(NZ):
        pltpu.make_async_copy(outs.at[0, zz], moe_out.at[:, zz * RS : (zz + 1) * RS], store_sem.at[3 + zz]).start()
        pltpu.make_async_copy(
            outs.at[1, zz], grad_tokens.at[:, zz * RS : (zz + 1) * RS], store_sem.at[3 + NZ + zz]
        ).start()

    @pl.when(core == 0)
    def _():
        for dz in range(1, NZ):
            src = zmod(z - dz)
            remote(gp.at[src], gp.at[src], g_send.at[dz, 0], g_recv.at[dz, 0], sibling).wait_recv()
        for dz in range(NZ):
            for dc in range(2):
                if dz or dc:
                    remote(gp.at[z], gp.at[z], g_send.at[dz, dc], g_recv.at[dz, dc], sibling).wait_send()

    @pl.when(core == 1)
    def _():
        for dz in range(NZ):
            src = zmod(z - dz)
            remote(gp.at[src], gp.at[src], g_send.at[dz, 1], g_recv.at[dz, 1], sibling).wait_recv()

    total = gp[0]
    for zz in range(1, NZ):
        total = total + gp[zz]
    grad_prob[...] = total

    for c in (store_g, store_u, store_d):
        c.wait()
    for zz in range(NZ):
        pltpu.make_async_copy(outs.at[0, zz], moe_out.at[:, zz * RS : (zz + 1) * RS], store_sem.at[3 + zz]).wait()
        pltpu.make_async_copy(
            outs.at[1, zz], grad_tokens.at[:, zz * RS : (zz + 1) * RS], store_sem.at[3 + NZ + zz]
        ).wait()
    for c in pending:
        c.wait_send()

    @pl.when(core == 0)
    def _():
        remote(w_gate.at[0], wgu.at[:, 0:H], wpre_sem.at[0], wpre_sem.at[2], sibling).wait_send()
        remote(w_up.at[0], wgu.at[:, 2 * H : 3 * H], wpre_sem.at[1], wpre_sem.at[3], sibling).wait_send()
        remote(gpre.at[:, 0:H], gpre.at[:, 0:H], act_sem.at[0], act_sem.at[2], sibling).wait_send()
        remote(gpre.at[:, 2 * H : 3 * H], gpre.at[:, 2 * H : 3 * H], act_sem.at[1], act_sem.at[3], sibling).wait_send()

    @pl.when(core == 1)
    def _():
        remote(w_down.at[0], wd.at[H : 2 * H, :], wpre_sem.at[0], wpre_sem.at[2], sibling).wait_send()
        remote(hid.at[:, H : 2 * H], hid.at[:, H : 2 * H], act_sem.at[0], act_sem.at[2], sibling).wait_send()


def per_device(tokens, assignment, route_weight, cotangent, w_gate, w_up, w_down):
    hbm = pl.BlockSpec(memory_space=pl.ANY)
    vmem = pl.BlockSpec(memory_space=pltpu.VMEM)
    dma = pltpu.SemaphoreType.DMA
    res = pl.pallas_call(
        kernel,
        out_shape=(
            jax.ShapeDtypeStruct((TOK, D), BF16),
            jax.ShapeDtypeStruct((TOK, D), BF16),
            jax.ShapeDtypeStruct((8, TOK), F32),
            jax.ShapeDtypeStruct((1, D, H), BF16),
            jax.ShapeDtypeStruct((1, D, H), BF16),
            jax.ShapeDtypeStruct((1, H, D), BF16),
        ),
        in_specs=[hbm, vmem, vmem, hbm, hbm, hbm, hbm],
        out_specs=(hbm, hbm, vmem, hbm, hbm, hbm),
        scratch_shapes=[
            pltpu.VMEM((TOK, D), BF16),
            pltpu.VMEM((TOK, RS), BF16),
            pltpu.VMEM((D, 4 * H), BF16),
            pltpu.VMEM((2 * H, D), BF16),
            pltpu.VMEM((SLOTS, KS), BF16),
            pltpu.VMEM((ND, SLOTS, KS), BF16),
            pltpu.VMEM((2, NK, SLOTS, KS), BF16),
            pltpu.VMEM((SLOTS, 2 * H), F32),
            pltpu.VMEM((SLOTS, H), F32),
            pltpu.VMEM((SLOTS, 2 * H), BF16),
            pltpu.VMEM((SLOTS, 4 * H), BF16),
            pltpu.VMEM((NZ, SLOTS, RS), BF16),
            pltpu.VMEM((4, SLOTS, RS), BF16),
            pltpu.VMEM((4, SLOTS, RS), BF16),
            pltpu.VMEM((2, SLOTS, RS), BF16),
            pltpu.VMEM((NZ, 8, TOK), F32),
            pltpu.VMEM((2, NZ, TOK, RS), BF16),
            pltpu.VMEM((D, H), BF16),
            pltpu.VMEM((D, H), BF16),
            pltpu.VMEM((H, D), BF16),
            dma((5,)), dma((4,)), dma((3 + 2 * NZ,)),
            dma((E - 1,)), dma((E - 1,)), dma((E - 1,)), dma((E - 1,)),
            dma((2, 4, 2)), dma((2, 4, 2)), dma((NZ, 2)), dma((NZ, 2)), dma((2,)),
            dma((4,)), dma((2, 4, 2)), dma((2, 4, 2)), dma((E, 2)), dma((E, 2)),
            dma((2, 4, 2)), dma((2, 4, 2)), dma((NZ, 2)), dma((NZ, 2)), dma((NZ, 2)), dma((NZ, 2)),
        ],
        compiler_params=pltpu.CompilerParams(
            collective_id=0, has_side_effects=True, vmem_limit_bytes=60 * 1024 * 1024
        ),
    )(tokens, assignment, route_weight, cotangent, w_gate, w_up, w_down)
    moe_out, grad_tokens, prob, grad_gate, grad_up, grad_down = res
    return (moe_out, grad_tokens, prob[0:2].T, grad_gate, grad_up, grad_down)


def solution(mesh):
    return jax.shard_map(
        per_device,
        mesh=mesh,
        in_specs=(
            P("expert", None),
            P("expert", None),
            P("expert", None),
            P("expert", None),
            P("expert", None, "fsdp"),
            P("expert", None, "fsdp"),
            P("expert", "fsdp", None),
        ),
        out_specs=(
            P("expert", None),
            P("expert", None),
            P("expert", None),
            P("expert", None, "fsdp"),
            P("expert", None, "fsdp"),
            P("expert", "fsdp", None),
        ),
        check_vma=False,
    )
```

time: 468 us -> 118 us (0.25); the launches traced: 462 us -> 117 us
  waiting for transfers between devices: 207 us -> 0 us
  Pallas kernels: 0 us -> 104 us
  starting transfers between devices: 84.5 us -> 0 us
  blocking collectives: 83.1 us -> 0 us
  matrix products: 44.1 us -> 0 us
  between operations: 15.1 us -> 0.65 us
  local copies, waits for them, and re-layouts: 25.5 us -> 12.3 us
    all_gather x2 -> x0, waiting for transfers between devices: 125 us -> none  [return_rows(): summed = lax.all_gather(shares, 'fsdp', axis=0, tiled=True)]
    pallas_call x0 -> x1, Pallas kernels: none -> 104 us  [per_device(): pl.pallas_call(kernel, out_shape=(jax.ShapeDtypeStruct((TOK, D), BF16), j...]
    unnamed x1 -> x0, blocking collectives: 83.1 us -> none
    unnamed x16 -> x0, starting transfers between devices: 65.1 us -> none
    all_to_all x4 -> x0, waiting for transfers between devices: 64.9 us -> none  [the longest x2 49.5 us: spread(): lax.all_to_all(blocks, 'expert', split_axis=0, concat_axis=0, tiled=True)]
    dot_general x16 -> x0, matrix products: 44.1 us -> none  [the longest x1 3.87 us: per_device(): jnp.dot(gathered.T, grad_pre_gate, preferred_element_type=jnp.float32)]
    all_to_all x4 -> x0, starting transfers between devices: 19.3 us -> none  [the longest x2 10.4 us: spread(): lax.all_to_all(blocks, 'expert', split_axis=0, concat_axis=0, tiled=True)]
    unnamed x18 -> x0, waiting for transfers between devices: 17.2 us -> none
  transfers between devices with their start and end apart: 22 -> 0, of which waited for: 10 -> 0; matrix products, arithmetic and copies ran while one was open for 9% -> 0% of each run, Pallas kernels for 0% -> 0%
where the time goes in v1:
time: 118 us; the launch traced here: 117 us
  Pallas kernels  104 us (88%)
  local copies, waits for them, and re-layouts  12.3 us (10%)
    pallas_call x1, Pallas kernels, per_device(): pl.pallas_call(kernel, out_shape=(jax.ShapeDtypeStruct((TOK, D), BF16), j...  104 us
    unnamed x15, local copies, waits for them, and re-layouts  11 us

profile of v1, /device:TPU:1, one launch (start us, length us, event | category | flops | bytes accessed | tf_op | source)
XLA Modules:
  0.0 117.3 jit_solution(2102590902366348520)
XLA Ops:
  0.6 1.4 %copy.13.assignment = s32[128,2]{1,0:T(8,128)} copy(s32[128,2]{0,1:T(2,128)} %param.8) | data formatting | bytes 2048 | tf_op args[1]
  2.0 1.4 %copy.14.weight = f32[128,2]{1,0:T(8,128)} copy(f32[128,2]{0,1:T(2,128)} %param.9) | data formatting | bytes 2048 | tf_op args[2]
  3.5 104.4 %shard_map.118 = (bf16[128,3072]{1,0:T(8,128)(2,1)}, bf16[128,3072]{1,0:T(8,128)(2,1)}, f32[8,128]{1,0:T(8,128)}, bf16[1,3072,256]{2,1,0:T(8,128)(2,1)}, bf16[1,...) custom-call(bf16[128,3072]{1,0:T(8,128)(2,1)} %tokens.1, s32[128,2]{1,0:T(8,128)} %copy.13.assignment, ...), custom_call_target="tpu_custom_call" | custom-call | tf_op jit(solution)/shard_map/pallas_call | solution.py:442
  107.9 0.0 copy-start.3
  107.9 1.3 %slice_bitcast_fusion = f32[128,2]{0,1:T(2,128)} fusion(f32[8,128]{1,0:T(8,128)} %get-tuple-element.14), kind=kLoop, calls=%fused_computation | loop fusion | bytes 2048 | tf_op jit(solution)/shard_map/transpose | solution.py:486
  109.2 0.0 copy-start.2
  109.2 2.2 %copy.20 = bf16[128,3072]{1,0:T(8,128)(2,1)} copy(bf16[128,3072]{1,0:T(8,128)(2,1)} %get-tuple-element.24) | data formatting | bytes 1572864
  111.4 0.0 copy-done.3
  111.4 0.9 copy.21
  112.3 0.0 copy-done.2
  112.3 0.0 copy-start.1
  112.3 1.1 copy.22
  113.4 0.8 copy-done.1
  114.2 0.0 copy-start
  114.2 1.1 copy.23
  115.4 0.8 copy-done
  116.2 1.1 copy.24
Async XLA Ops:
  107.9 3.5 %copy-start.3 = (bf16[128,3072]{1,0:T(8,128)(2,1)S(1)}, bf16[128,3072]{1,0:T(8,128)(2,1)}, u32[]{:S(2)}) copy-start(bf16[128,3072]{1,0:T(8,128)(2,1)} %get-tuple-element.25) | copy-start | bytes 2359300
  109.2 3.1 %copy-start.2 = (bf16[1,3072,256]{2,1,0:T(8,128)(2,1)S(1)}, bf16[1,3072,256]{2,1,0:T(8,128)(2,1)}, u32[]{:S(2)}) copy-start(bf16[1,3072,256]{2,1,0:T(8,128)(2,1)} %get-tuple-element.27) | copy-start | bytes 4718596
  112.3 2.0 %copy-start.1 = (bf16[1,3072,256]{2,1,0:T(8,128)(2,1)S(1)}, bf16[1,3072,256]{2,1,0:T(8,128)(2,1)}, u32[]{:S(2)}) copy-start(bf16[1,3072,256]{2,1,0:T(8,128)(2,1)} %get-tuple-element.28) | copy-start | bytes 4718596
  114.2 2.0 %copy-start = (bf16[1,256,3072]{2,1,0:T(8,128)(2,1)S(1)}, bf16[1,256,3072]{2,1,0:T(8,128)(2,1)}, u32[]{:S(2)}) copy-start(bf16[1,256,3072]{2,1,0:T(8,128)(2,1)} %get-tuple-element.29) | copy-start | bytes 4718596

commit v2 on v1

v2 whole, which is shorter than its diff:
```python
import jax
import jax.numpy as jnp
from jax import lax
from jax.experimental import pallas as pl
from jax.experimental.pallas import tpu as pltpu
from jax.sharding import PartitionSpec as P

MESH = pl.DeviceIdType.MESH
BF16 = jnp.bfloat16
F32 = jnp.float32
NT = (((1,), (1,)), ((), ()))
TN = (((0,), (0,)), ((), ()))

E = 8
NZ = 8
CAP = 48
TOK = 128
SLOTS = E * CAP
D = 3072
H = 256
HALF = SLOTS // 2
KS = 256
NK = D // KS
ND = NK - NZ
RS = D // NZ
QC = 128
NQ = RS // QC
NP = 4


def rows_of(index, size):
    return pl.ds(pl.multiple_of(index * size, size), size)


def kernel(
    tokens, assign_t, weight_t, cotangent, w_gate, w_up, w_down,
    outs, prob, gg, gu, gd,
    acts_s, acts_d, cot_part, wgu, wd, send_s, send_d, xd, acc_gu, acc_h, hid, gpre,
    part, rp, rm, rc, gp,
    load_sem, wpre_sem,
    a_send, a_recv, d_send, d_recv, ring_send, ring_recv, sib_send, sib_recv, dsib_sem,
    act_sem, rs_send, rs_recv, c_send, c_recv, o_send, o_recv, osib_send, osib_recv, g_send, g_recv,
):
    e = lax.axis_index("expert")
    f = lax.axis_index("fsdp")
    core = lax.rem(f, 2)
    z = lax.rem(lax.div(f, 2), NZ)
    yh = lax.div(f, 2 * NZ)
    t = core
    other = 1 - core

    def dev(e_, yh_, z_, c_):
        return (e_, yh_ * (2 * NZ) + z_ * 2 + c_)

    sibling = dev(e, yh, z, 1 - core)
    up = dev(e, yh, lax.rem(z + 1, NZ), core)
    down = dev(e, yh, lax.rem(z + NZ - 1, NZ), core)

    def zmod(v):
        return lax.rem(v + 2 * NZ, NZ)

    pending = []

    def remote(src, dst, ss, rs, device):
        return pltpu.make_async_remote_copy(
            src_ref=src, dst_ref=dst, send_sem=ss, recv_sem=rs, device_id=device, device_id_type=MESH
        )

    def send(src, dst, ss, rs, device):
        c = remote(src, dst, ss, rs, device)
        c.start()
        pending.append(c)

    def arrived(dst, ss, rs):
        remote(dst, dst, ss, rs, sibling).wait_recv()

    loads = []
    for c, source in enumerate((tokens, cotangent)):
        loads.append((
            pltpu.make_async_copy(source.at[:, rows_of(z, KS)], acts_s, load_sem.at[0]),
            pltpu.make_async_copy(source.at[:, NZ * KS :], acts_d, load_sem.at[5]),
        ))

        @pl.when(core == c)
        def _(c=c):
            loads[c][0].start()
            loads[c][1].start()

    own_g = pltpu.make_async_copy(w_gate.at[0], wgu.at[:, rows_of(core, H)], load_sem.at[1])
    own_u = pltpu.make_async_copy(w_up.at[0], wgu.at[:, rows_of(core + 2, H)], load_sem.at[2])
    own_d = pltpu.make_async_copy(w_down.at[0], wd.at[rows_of(core, H), :], load_sem.at[3])
    own_c = pltpu.make_async_copy(cotangent.at[:, rows_of(z, RS)], cot_part, load_sem.at[4])
    for c in (own_g, own_u, own_d, own_c):
        c.start()

    barrier = pltpu.get_barrier_semaphore()

    def greet(device):
        pl.semaphore_signal(barrier, inc=1, device_id=device, device_id_type=MESH)

    for i in range(E):
        for dy in range(2):
            if i or dy:
                greet(dev(lax.rem(e + i, E), lax.rem(yh + dy, 2), z, core))
    for dz in range(NZ):
        for dc in range(2):
            if dz or dc:
                greet(dev(e, yh, lax.rem(z + dz, NZ), lax.rem(core + dc, 2)))

    a0 = assign_t[0:1, :]
    a1 = assign_t[1:2, :]
    w0_row = weight_t[0:1, :]
    w1_row = weight_t[1:2, :]
    expert = lax.broadcasted_iota(jnp.int32, (8, TOK), 0)
    hot0 = (expert == a0).astype(F32)
    hot1 = (expert == a1).astype(F32)
    lane = lax.broadcasted_iota(jnp.int32, (TOK, TOK), 1)
    row = lax.broadcasted_iota(jnp.int32, (TOK, TOK), 0)
    before = (row < lane).astype(BF16)
    count = jnp.dot((hot0 + hot1).astype(BF16), before, preferred_element_type=F32)
    slot0 = a0 * CAP + jnp.sum(hot0 * count, axis=0, keepdims=True).astype(jnp.int32)
    slot1 = a1 * CAP + jnp.sum(hot1 * count, axis=0, keepdims=True).astype(jnp.int32)
    slot = lax.broadcasted_iota(jnp.int32, (SLOTS, TOK), 0)
    spread0 = (slot == slot0).astype(F32)
    spread1 = (slot == slot1).astype(F32)
    spread = (spread0 + spread1).astype(BF16)
    slot_weight = jnp.sum(spread0 * w0_row + spread1 * w1_row, axis=1, keepdims=True)
    is_x = core == 0
    scale_in = jnp.where(is_x, 1.0, slot_weight)

    def dispatch(cols):
        return (scale_in * jnp.dot(spread, cols, preferred_element_type=F32)).astype(BF16)

    for c in range(2):

        @pl.when(core == c)
        def _(c=c):
            loads[c][0].wait()

    own_rows = rows_of(e, CAP)
    send_s[...] = dispatch(acts_s[...])
    xd[t, z, own_rows, :] = send_s[own_rows, :]

    pl.semaphore_wait(barrier, 2 * E - 1 + 2 * NZ - 1)

    for i in range(1, E):
        j = lax.rem(e + i, E)
        send(
            send_s.at[rows_of(j, CAP), :], xd.at[t, z, own_rows, :],
            a_send.at[i - 1], a_recv.at[i - 1], dev(j, yh, z, core),
        )

    @pl.when(core == 0)
    def _():
        remote(w_gate.at[0], wgu.at[:, 0:H], wpre_sem.at[0], wpre_sem.at[2], sibling).start()
        remote(w_up.at[0], wgu.at[:, 2 * H : 3 * H], wpre_sem.at[1], wpre_sem.at[3], sibling).start()

    @pl.when(core == 1)
    def _():
        remote(w_down.at[0], wd.at[H : 2 * H, :], wpre_sem.at[0], wpre_sem.at[2], sibling).start()

    for c in range(2):

        @pl.when(core == c)
        def _(c=c):
            loads[c][1].wait()

    for k in range(ND):
        send_d[k] = dispatch(acts_d[:, k * KS : (k + 1) * KS])
    for k in range(ND):
        xd[t, NZ + k, own_rows, :] = send_d[k, own_rows, :]
    acc_gu[...] = jnp.zeros_like(acc_gu)
    acc_h[...] = jnp.zeros_like(acc_h)
    pick0 = spread0.T.astype(BF16)
    pick1 = spread1.T.astype(BF16)
    w0 = jnp.broadcast_to(w0_row, (TOK, TOK)).T[:, 0:1]
    w1 = jnp.broadcast_to(w1_row, (TOK, TOK)).T[:, 0:1]
    on0 = jnp.where(is_x, w0, 1.0)
    on1 = jnp.where(is_x, w1, 1.0)
    for c in (own_g, own_u, own_d, own_c):
        c.wait()

    def gather(view, parts, sems):
        s_send, s_recv, b_send, b_recv = sems

        for s in range(5):
            for p in range(parts):
                for way, nxt, sign in ((0, up, -1), (1, down, 1)):
                    split = (p < parts // 2) == (way == 0)
                    if s == 4 and not split:
                        continue
                    ref = view(t, zmod(z + sign * s), p)
                    if s > 0:
                        arrived(ref, s_send.at[way, s - 1, p], s_recv.at[way, s - 1, p])
                    if s < 3 or (s == 3 and split):
                        send(ref, ref, s_send.at[way, s, p], s_recv.at[way, s, p], nxt)
                    if s > 0 or way == 0:
                        d = (sign * s) % NZ
                        send(ref, ref, b_send.at[d, p], b_recv.at[d, p], sibling)
            yield

    def sib_arrived(view, parts, sems, d):
        for p in range(parts):
            arrived(view(other, zmod(z + d), p), sems[2].at[d % NZ, p], sems[3].at[d % NZ, p])

    def xd_view(kind, zz, p):
        return xd.at[kind, zz, p * (SLOTS // NP) : (p + 1) * (SLOTS // NP), :]

    mine_g = rows_of(core, H)
    mine_u = rows_of(core + 2, H)

    def add_x(k):
        kr = rows_of(k, KS)
        acc_gu[:, 0:H] += jnp.dot(xd[0, k], wgu[kr, mine_g], preferred_element_type=F32)
        acc_gu[:, H : 2 * H] += jnp.dot(xd[0, k], wgu[kr, mine_u], preferred_element_type=F32)

    def add_y(k):
        acc_h[...] += lax.dot_general(xd[1, k], wd[mine_g, rows_of(k, KS)], NT, preferred_element_type=F32)

    def products(kind, count, index):
        @pl.when(kind == 0)
        def _():
            @pl.loop(0, count)
            def _(i):
                add_x(index(i))

        @pl.when(kind == 1)
        def _():
            @pl.loop(0, count)
            def _(i):
                add_y(index(i))

    def pair(s):
        return lambda i: zmod(z - s + 2 * s * i)

    ring_sems = (ring_send, ring_recv, sib_send, sib_recv)
    for i in range(1, E):
        src = rows_of(lax.rem(e + E - i, E), CAP)
        arrived(xd.at[t, z, src, :], a_send.at[i - 1], a_recv.at[i - 1])
    ring = gather(xd_view, NP, ring_sems)
    next(ring)
    for i in range(1, E):
        j = lax.rem(e + i, E)
        send(
            send_d.at[:, rows_of(j, CAP), :], xd.at[t, NZ:NK, own_rows, :],
            d_send.at[i - 1], d_recv.at[i - 1], dev(j, yh, z, core),
        )
    products(t, 1, lambda i: z)
    next(ring)
    products(t, 2, pair(1))
    sib_arrived(xd_view, NP, ring_sems, 0)
    products(other, 1, lambda i: z)
    next(ring)
    products(t, 2, pair(2))
    for d in (-1, 1):
        sib_arrived(xd_view, NP, ring_sems, d)
    products(other, 2, pair(1))
    next(ring)
    products(t, 2, pair(3))
    for d in (-2, 2):
        sib_arrived(xd_view, NP, ring_sems, d)
    products(other, 2, pair(2))
    for i in range(1, E):
        src = rows_of(lax.rem(e + E - i, E), CAP)
        arrived(xd.at[t, NZ:NK, src, :], d_send.at[i - 1], d_recv.at[i - 1])
    send(xd.at[t, NZ:NK], xd.at[t, NZ:NK], dsib_sem.at[0], dsib_sem.at[1], sibling)
    products(t, ND, lambda i: NZ + i)
    for d in (-3, 3):
        sib_arrived(xd_view, NP, ring_sems, d)
    products(other, 2, pair(3))
    next(ring)
    arrived(xd.at[other, NZ:NK], dsib_sem.at[0], dsib_sem.at[1])
    products(other, ND, lambda i: NZ + i)
    products(t, 1, lambda i: zmod(z + 4))
    sib_arrived(xd_view, NP, ring_sems, 4)
    products(other, 1, lambda i: zmod(z + 4))

    @pl.loop(0, E)
    def _(b):
        r = rows_of(b, CAP)
        pre_gate = acc_gu[r, 0:H]
        pre_up = acc_gu[r, H : 2 * H]
        grad_hidden = acc_h[r, :]
        sigma = jax.nn.sigmoid(pre_gate)
        silu = pre_gate * sigma
        hid[r, mine_g] = (silu * pre_up).astype(BF16)
        gpre[r, mine_g] = (grad_hidden * pre_up * sigma * (1.0 + pre_gate * (1.0 - sigma))).astype(BF16)
        gpre[r, mine_u] = (grad_hidden * silu).astype(BF16)

    @pl.when(core == 0)
    def _():
        cg = remote(gpre.at[:, 0:H], gpre.at[:, 0:H], act_sem.at[0], act_sem.at[2], sibling)
        cu = remote(gpre.at[:, 2 * H : 3 * H], gpre.at[:, 2 * H : 3 * H], act_sem.at[1], act_sem.at[3], sibling)
        cg.start()
        cu.start()
        arrived(wd.at[H : 2 * H, :], wpre_sem.at[0], wpre_sem.at[2])
        arrived(hid.at[:, H : 2 * H], act_sem.at[0], act_sem.at[2])

    @pl.when(core == 1)
    def _():
        ch = remote(hid.at[:, H : 2 * H], hid.at[:, H : 2 * H], act_sem.at[0], act_sem.at[2], sibling)
        ch.start()
        arrived(wgu.at[:, 0:H], wpre_sem.at[0], wpre_sem.at[2])
        arrived(wgu.at[:, 2 * H : 3 * H], wpre_sem.at[1], wpre_sem.at[3])
        arrived(gpre.at[:, 0:H], act_sem.at[0], act_sem.at[2])
        arrived(gpre.at[:, 2 * H : 3 * H], act_sem.at[1], act_sem.at[3])

    def term(zd):
        cols = rows_of(zd, RS)

        def keep(v):
            for q in range(NQ):
                part[q, zd] = v[:, q * QC : (q + 1) * QC].astype(BF16)

        @pl.when(core == 0)
        def _():
            keep(jnp.dot(hid[...], wd[:, cols], preferred_element_type=F32))

        @pl.when(core == 1)
        def _():
            keep(lax.dot_general(gpre[...], wgu[cols, :], NT, preferred_element_type=F32))

    def weight_grads(first, last):
        @pl.loop(first, last)
        def _(k):
            kr = rows_of(k, KS)
            g = lax.dot_general(xd[0, k], gpre[:, mine_g], TN, preferred_element_type=F32)
            gg[kr, :] = g.astype(BF16)
            u = lax.dot_general(xd[0, k], gpre[:, mine_u], TN, preferred_element_type=F32)
            gu[kr, :] = u.astype(BF16)
            w = lax.dot_general(hid[:, mine_g], xd[1, k], TN, preferred_element_type=F32)
            gd[:, kr] = w.astype(BF16)

    land = (rp, rm)

    def half(h):
        return slice(h * HALF, (h + 1) * HALF)

    def target(way, s):
        return zmod(z + 4 - s) if way == 0 else zmod(z - 4 + s)

    probs = []

    def back(q):
        def rs_start(way, s, h):
            send(
                part.at[q, target(way, s), half(h), :], land[way].at[q, s, half(h), :],
                rs_send.at[q, way * 4 + s, h], rs_recv.at[q, way * 4 + s, h], up if way == 0 else down,
            )

        def rs_arrived(way, s, h):
            arrived(land[way].at[q, s, half(h), :], rs_send.at[q, way * 4 + s, h], rs_recv.at[q, way * 4 + s, h])

        def rs_add(way, s, h):
            zd = target(way, s + 1)
            part[q, zd, half(h), :] = (
                part[q, zd, half(h), :].astype(F32) + land[way][q, s, half(h), :].astype(F32)
            ).astype(BF16)

        if q == 0:
            term(zmod(z + 4))
        rs_start(0, 0, 0)
        rs_start(1, 0, 1)
        if q == 0:
            term(zmod(z + 3))
        rs_start(0, 1, 1)
        if q == 0:
            term(zmod(z + 5))
        rs_start(1, 1, 0)
        yield
        for way, h in ((0, 0), (1, 1)):
            rs_arrived(way, 0, h)
            rs_add(way, 0, h)
            rs_start(way, 1, h)
        yield
        for s in (1, 2):
            for way, h in ((0, 1), (1, 0), (0, 0), (1, 1)):
                rs_arrived(way, s, h)
                rs_add(way, s, h)
                rs_start(way, s + 1, h)
            yield
        for h in range(2):
            for way in range(2):
                rs_arrived(way, 3, h)
            part[q, z, half(h), :] = (
                part[q, z, half(h), :].astype(F32)
                + rp[q, 3, half(h), :].astype(F32)
                + rm[q, 3, half(h), :].astype(F32)
            ).astype(BF16)
        rc[q, yh, own_rows, :] = part[q, z, own_rows, :]
        for i in range(E):
            for dy in range(2):
                if i or dy:
                    b = lax.rem(e + i, E)
                    send(
                        part.at[q, z, rows_of(b, CAP), :], rc.at[q, yh, own_rows, :],
                        c_send.at[q, i * 2 + dy], c_recv.at[q, i * 2 + dy], dev(b, lax.rem(yh + dy, 2), z, core),
                    )
        yield
        for i in range(E):
            for dy in range(2):
                if i or dy:
                    src = rows_of(lax.rem(e + E - i, E), CAP)
                    arrived(
                        rc.at[q, lax.rem(yh + dy, 2), src, :], c_send.at[q, i * 2 + dy], c_recv.at[q, i * 2 + dy]
                    )
        summed = (rc[q, 0].astype(F32) + rc[q, 1].astype(F32)).astype(BF16)
        out0 = jnp.dot(pick0, summed, preferred_element_type=F32)
        out1 = jnp.dot(pick1, summed, preferred_element_type=F32)
        outs[t, :, pl.ds(pl.multiple_of(z * RS + q * QC, QC), QC)] = (on0 * out0 + on1 * out1).astype(BF16)

        def out_view(kind, zz, p):
            return outs.at[
                kind, p * (TOK // 2) : (p + 1) * (TOK // 2), pl.ds(pl.multiple_of(zz * RS + q * QC, QC), QC)
            ]

        sems = (o_send.at[q], o_recv.at[q], osib_send.at[q], osib_recv.at[q])
        steps = gather(out_view, 2, sems)
        next(steps)
        cot = cot_part[:, q * QC : (q + 1) * QC].astype(F32)
        probs.append((jnp.sum(cot * out0, axis=1, keepdims=True), jnp.sum(cot * out1, axis=1, keepdims=True)))
        if q == NQ - 1:
            p0 = sum(v[0] for v in probs)
            p1 = sum(v[1] for v in probs)
            both = jnp.where(lane == 0, p0, 0.0) + jnp.where(lane == 1, p1, 0.0)

            @pl.when(core == 0)
            def _():
                gp[z] = both.T[0:8, :]
                for dz in range(NZ):
                    for dc in range(2):
                        if dz or dc:
                            remote(
                                gp.at[z], gp.at[z], g_send.at[dz, dc], g_recv.at[dz, dc],
                                dev(e, yh, lax.rem(z + dz, NZ), dc),
                            ).start()

        yield
        for _ in steps:
            yield
        for d in range(NZ):
            sib_arrived(out_view, 2, sems, d)
        yield

    q0, q1, q2 = (back(q) for q in range(NQ))
    next(q0)
    next(q1)

    @pl.loop(0, 5)
    def _(i):
        term(zmod(z + 6 + i))

    next(q0)
    next(q2)
    weight_grads(0, 4)
    next(q0)
    next(q1)
    weight_grads(4, 8)
    next(q0)
    next(q1)
    next(q2)
    weight_grads(8, 12)
    next(q0)
    next(q1)
    next(q2)
    for turn in ((q2, q1, q0), (q2, q0, q1), (q0, q1, q2), (q0, q1, q2), (q0, q1, q2), (q0, q1, q2), (q1, q2), (q2,)):
        for q in turn:
            next(q)

    @pl.when(core == 0)
    def _():
        for dz in range(1, NZ):
            src = zmod(z - dz)
            remote(gp.at[src], gp.at[src], g_send.at[dz, 0], g_recv.at[dz, 0], sibling).wait_recv()
        for dz in range(NZ):
            for dc in range(2):
                if dz or dc:
                    remote(gp.at[z], gp.at[z], g_send.at[dz, dc], g_recv.at[dz, dc], sibling).wait_send()

    @pl.when(core == 1)
    def _():
        for dz in range(NZ):
            src = zmod(z - dz)
            remote(gp.at[src], gp.at[src], g_send.at[dz, 1], g_recv.at[dz, 1], sibling).wait_recv()

    total = gp[0]
    for zz in range(1, NZ):
        total = total + gp[zz]
    prob[...] = total[0:2, :]

    for c in pending:
        c.wait_send()

    @pl.when(core == 0)
    def _():
        remote(w_gate.at[0], wgu.at[:, 0:H], wpre_sem.at[0], wpre_sem.at[2], sibling).wait_send()
        remote(w_up.at[0], wgu.at[:, 2 * H : 3 * H], wpre_sem.at[1], wpre_sem.at[3], sibling).wait_send()
        remote(gpre.at[:, 0:H], gpre.at[:, 0:H], act_sem.at[0], act_sem.at[2], sibling).wait_send()
        remote(gpre.at[:, 2 * H : 3 * H], gpre.at[:, 2 * H : 3 * H], act_sem.at[1], act_sem.at[3], sibling).wait_send()

    @pl.when(core == 1)
    def _():
        remote(w_down.at[0], wd.at[H : 2 * H, :], wpre_sem.at[0], wpre_sem.at[2], sibling).wait_send()
        remote(hid.at[:, H : 2 * H], hid.at[:, H : 2 * H], act_sem.at[0], act_sem.at[2], sibling).wait_send()


def store(outs, prob, gg, gu, gd, moe_out, grad_tokens, grad_prob, grad_gate, grad_up, grad_down, sem):
    copies = []
    for i, (src, dst) in enumerate((
        (gg, grad_gate.at[0]), (gu, grad_up.at[0]), (gd, grad_down.at[0]),
        (outs.at[0], moe_out), (outs.at[1], grad_tokens), (prob, grad_prob),
    )):
        copies.append(pltpu.make_async_copy(src, dst, sem.at[i]))
    for c in copies:
        c.start()
    for c in copies:
        c.wait()


def per_device(tokens, assignment, route_weight, cotangent, w_gate, w_up, w_down):
    hbm = pl.BlockSpec(memory_space=pl.ANY)
    vmem = pl.BlockSpec(memory_space=pltpu.VMEM)
    dma = pltpu.SemaphoreType.DMA
    held = pl.pallas_call(
        kernel,
        out_shape=(
            pltpu.VMEM((2, TOK, D), BF16),
            pltpu.VMEM((2, TOK), F32),
            pltpu.VMEM((D, H), BF16),
            pltpu.VMEM((D, H), BF16),
            pltpu.VMEM((H, D), BF16),
        ),
        in_specs=[hbm, vmem, vmem, hbm, hbm, hbm, hbm],
        out_specs=(vmem,) * 5,
        scratch_shapes=[
            pltpu.VMEM((TOK, KS), BF16),
            pltpu.VMEM((TOK, ND * KS), BF16),
            pltpu.VMEM((TOK, RS), BF16),
            pltpu.VMEM((D, 4 * H), BF16),
            pltpu.VMEM((2 * H, D), BF16),
            pltpu.VMEM((SLOTS, KS), BF16),
            pltpu.VMEM((ND, SLOTS, KS), BF16),
            pltpu.VMEM((2, NK, SLOTS, KS), BF16),
            pltpu.VMEM((SLOTS, 2 * H), F32),
            pltpu.VMEM((SLOTS, H), F32),
            pltpu.VMEM((SLOTS, 2 * H), BF16),
            pltpu.VMEM((SLOTS, 4 * H), BF16),
            pltpu.VMEM((NQ, NZ, SLOTS, QC), BF16),
            pltpu.VMEM((NQ, 4, SLOTS, QC), BF16),
            pltpu.VMEM((NQ, 4, SLOTS, QC), BF16),
            pltpu.VMEM((NQ, 2, SLOTS, QC), BF16),
            pltpu.VMEM((NZ, 8, TOK), F32),
            dma((6,)), dma((4,)),
            dma((E - 1,)), dma((E - 1,)), dma((E - 1,)), dma((E - 1,)),
            dma((2, 4, NP)), dma((2, 4, NP)), dma((NZ, NP)), dma((NZ, NP)), dma((2,)),
            dma((4,)), dma((NQ, 8, 2)), dma((NQ, 8, 2)), dma((NQ, 2 * E)), dma((NQ, 2 * E)),
            dma((NQ, 2, 4, 2)), dma((NQ, 2, 4, 2)), dma((NQ, NZ, 2)), dma((NQ, NZ, 2)),
            dma((NZ, 2)), dma((NZ, 2)),
        ],
        compiler_params=pltpu.CompilerParams(
            collective_id=0, has_side_effects=True, vmem_limit_bytes=50 * 1024 * 1024
        ),
    )(tokens, assignment.T, route_weight.T, cotangent, w_gate, w_up, w_down)
    moe_out, grad_tokens, grad_prob, grad_gate, grad_up, grad_down = pl.pallas_call(
        store,
        out_shape=(
            jax.ShapeDtypeStruct((TOK, D), BF16),
            jax.ShapeDtypeStruct((TOK, D), BF16),
            jax.ShapeDtypeStruct((2, TOK), F32),
            jax.ShapeDtypeStruct((1, D, H), BF16),
            jax.ShapeDtypeStruct((1, D, H), BF16),
            jax.ShapeDtypeStruct((1, H, D), BF16),
        ),
        in_specs=[vmem] * 5,
        out_specs=(hbm,) * 6,
        scratch_shapes=[dma((6,))],
        compiler_params=pltpu.CompilerParams(vmem_limit_bytes=16 * 1024 * 1024),
    )(*held)
    return (moe_out, grad_tokens, grad_prob.T, grad_gate, grad_up, grad_down)


def solution(mesh):
    return jax.shard_map(
        per_device,
        mesh=mesh,
        in_specs=(
            P("expert", None),
            P("expert", None),
            P("expert", None),
            P("expert", None),
            P("expert", None, "fsdp"),
            P("expert", None, "fsdp"),
            P("expert", "fsdp", None),
        ),
        out_specs=(
            P("expert", None),
            P("expert", None),
            P("expert", None),
            P("expert", None, "fsdp"),
            P("expert", None, "fsdp"),
            P("expert", "fsdp", None),
        ),
        check_vma=False,
    )
```

time: 118 us -> 95.6 us (0.81)
  local copies, waits for them, and re-layouts: 12.3 us -> 0 us
  Pallas kernels: 104 us -> 94.8 us
    unnamed x15 -> x0, local copies, waits for them, and re-layouts: 11 us -> none
    pallas_call x1 -> x2, Pallas kernels: 104 us -> 94.8 us  [the longest x1 92.1 us: per_device(): pl.pallas_call(kernel, out_shape=(pltpu.VMEM((2, TOK, D), BF16), pltpu.VM...]
    transpose x1 -> x0, local copies, waits for them, and re-layouts: 1.31 us -> none  [per_device(): return (moe_out, grad_tokens, prob[0:2].T, grad_gate, grad_up, grad_down)]
where the time goes in v2:
time: 95.6 us; the launch traced here: 95.5 us
  Pallas kernels  94.8 us (99%)
    pallas_call x1, Pallas kernels, per_device(): pl.pallas_call(kernel, out_shape=(pltpu.VMEM((2, TOK, D), BF16), pltpu.VM...  92.1 us
    pallas_call x1, Pallas kernels, per_device(): pl.pallas_call(store, out_shape=(jax.ShapeDtypeStruct((TOK, D), BF16), ja...  2.73 us

profile of v2, /device:TPU:1, one launch (start us, length us, event | category | flops | bytes accessed | tf_op | source)
XLA Modules:
  0.0 95.5 jit_solution(17499394397896797325)
XLA Ops:
  0.6 92.1 %shard_map.118 = (bf16[2,128,3072]{2,1,0:T(8,128)(2,1)S(1)}, f32[2,128]{1,0:T(2,128)S(1)}, bf16[3072,256]{1,0:T(8,128)(2,1)S(1)}, bf16[3072,256]{1,0:T(8,128)(2,1)S(1)}, bf16[256,3072]{1,0:T(8,128)(2,1)S(1)}) custom-call(bf16[128,3072]{1,0:T(8,128)(2,1)} %tokens.1, s32[2,128]{1,0:T(2,128)} %bitcast.3, f32[2,128]{1,0:T(2,128)} %bitcast.4, ...), custom_call_target="tpu_custom_call" | custom-call | tf_op jit(solution)/shard_map/pallas_call | solution.py:524
  92.7 2.7 %shard_map.119 = (bf16[128,3072]{1,0:T(8,128)(2,1)}, bf16[128,3072]{1,0:T(8,128)(2,1)}, f32[2,128]{1,0:T(2,128)}, bf16[1,3072,256]{2,1,0:T(8,128)(2,1)}, bf16[1,...) custom-call(bf16[2,128,3072]{2,1,0:T(8,128)(2,1)S(1)} %get-tuple-element.17.outs, ...), custom_call_target="tpu_custom_call" | custom-call | tf_op jit(solution)/shard_map/pallas_call | solution.py:564

commit v3 on v0

v3 whole, which is shorter than its diff:
```python
import jax
import jax.numpy as jnp
from jax import lax
from jax.experimental import pallas as pl
from jax.experimental.pallas import tpu as pltpu
from jax.sharding import PartitionSpec as P

MESH = pl.DeviceIdType.MESH
BF16 = jnp.bfloat16
F32 = jnp.float32
NT = (((1,), (1,)), ((), ()))
TN = (((0,), (0,)), ((), ()))

E = 8
NZ = 8
CAP = 48
TOK = 128
SLOTS = E * CAP
D = 3072
H = 256
HALF = SLOTS // 2
KS = 256
NK = D // KS
ND = NK - NZ
RS = D // NZ
QC = 128
NQ = RS // QC
NP = 4


def rows_of(index, size):
    return pl.ds(pl.multiple_of(index * size, size), size)


def kernel(
    tokens, assign_t, weight_t, cotangent, w_gate, w_up, w_down,
    outs, prob, gg, gu, gd,
    acts_s, acts_d, cot_part, wgu, wd, send_s, send_d, xd, acc_gu, acc_h, hid, gpre,
    part, rp, rm, rc, gp, gp_sum,
    load_sem, wpre_sem,
    a_send, a_recv, d_send, d_recv, ring_send, ring_recv, sib_send, sib_recv, dsib_sem,
    act_sem, rs_send, rs_recv, c_send, c_recv, o_send, o_recv, osib_send, osib_recv, g_send, g_recv, gsum_sem,
):
    e = lax.axis_index("expert")
    f = lax.axis_index("fsdp")
    core = lax.rem(f, 2)
    z = lax.rem(lax.div(f, 2), NZ)
    yh = lax.div(f, 2 * NZ)

    def dev(e_, yh_, z_, c_):
        return (e_, yh_ * (2 * NZ) + z_ * 2 + c_)

    sibling = dev(e, yh, z, 1 - core)
    up = dev(e, yh, lax.rem(z + 1, NZ), core)
    down = dev(e, yh, lax.rem(z + NZ - 1, NZ), core)

    def zmod(v):
        return lax.rem(v + 2 * NZ, NZ)

    def remote(src, dst, ss, rs, device):
        return pltpu.make_async_remote_copy(
            src_ref=src, dst_ref=dst, send_sem=ss, recv_sem=rs, device_id=device, device_id_type=MESH
        )

    def arrived(dst, ss, rs):
        remote(dst, dst, ss, rs, sibling).wait_recv()

    loads = []
    for c, source in enumerate((tokens, cotangent)):
        loads.append((
            pltpu.make_async_copy(source.at[:, rows_of(z, KS)], acts_s, load_sem.at[0]),
            pltpu.make_async_copy(source.at[:, NZ * KS :], acts_d, load_sem.at[5]),
        ))

        @pl.when(core == c)
        def _(c=c):
            loads[c][0].start()
            loads[c][1].start()

    own_g = pltpu.make_async_copy(w_gate.at[0], wgu.at[:, rows_of(core, H)], load_sem.at[1])
    own_u = pltpu.make_async_copy(w_up.at[0], wgu.at[:, rows_of(core + 2, H)], load_sem.at[2])
    own_d = pltpu.make_async_copy(w_down.at[0], wd.at[rows_of(core, H), :], load_sem.at[3])
    own_c = pltpu.make_async_copy(cotangent.at[:, rows_of(z, RS)], cot_part, load_sem.at[4])
    for c in (own_g, own_u, own_d, own_c):
        c.start()

    barrier = pltpu.get_barrier_semaphore()

    def greet(device):
        pl.semaphore_signal(barrier, inc=1, device_id=device, device_id_type=MESH)

    greet(sibling)
    for i in range(E):
        for dy in range(2):
            if i or dy:
                greet(dev(lax.rem(e + i, E), lax.rem(yh + dy, 2), z, core))
    for dz in range(1, NZ):
        greet(dev(e, yh, lax.rem(z + dz, NZ), core))

    a0 = assign_t[0:1, :]
    a1 = assign_t[1:2, :]
    w0_row = weight_t[0:1, :]
    w1_row = weight_t[1:2, :]
    expert = lax.broadcasted_iota(jnp.int32, (8, TOK), 0)
    hot0 = (expert == a0).astype(F32)
    hot1 = (expert == a1).astype(F32)
    lane = lax.broadcasted_iota(jnp.int32, (TOK, TOK), 1)
    row = lax.broadcasted_iota(jnp.int32, (TOK, TOK), 0)
    before = (row < lane).astype(BF16)
    count = jnp.dot((hot0 + hot1).astype(BF16), before, preferred_element_type=F32)
    slot0 = a0 * CAP + jnp.sum(hot0 * count, axis=0, keepdims=True).astype(jnp.int32)
    slot1 = a1 * CAP + jnp.sum(hot1 * count, axis=0, keepdims=True).astype(jnp.int32)
    slot = lax.broadcasted_iota(jnp.int32, (SLOTS, TOK), 0)
    spread0 = (slot == slot0).astype(F32)
    spread1 = (slot == slot1).astype(F32)
    spread = (spread0 + spread1).astype(BF16)
    own_rows = rows_of(e, CAP)
    mine_g = rows_of(core, H)
    mine_u = rows_of(core + 2, H)
    land = (rp, rm)

    def half(h):
        return slice(h * HALF, (h + 1) * HALF)

    def target(way, s):
        return zmod(z + 4 - s) if way == 0 else zmod(z - 4 + s)

    def xd_view(kind, zz, p):
        return xd.at[kind, zz, p * (SLOTS // NP) : (p + 1) * (SLOTS // NP), :]

    ring_sems = (ring_send, ring_recv, sib_send, sib_recv)

    def sib_arrived(view, kind, parts, sems, d):
        for p in range(parts):
            arrived(view(kind, zmod(z + d), p), sems[2].at[d % NZ, p], sems[3].at[d % NZ, p])

    def add_x(k):
        kr = rows_of(k, KS)
        acc_gu[:, 0:H] += jnp.dot(xd[0, k], wgu[kr, mine_g], preferred_element_type=F32)
        acc_gu[:, H : 2 * H] += jnp.dot(xd[0, k], wgu[kr, mine_u], preferred_element_type=F32)

    def add_y(k):
        acc_h[...] += lax.dot_general(xd[1, k], wd[mine_g, rows_of(k, KS)], NT, preferred_element_type=F32)

    def add_pair(add, s):
        @pl.loop(0, 2)
        def _(i):
            add(zmod(z - s + 2 * s * i))

    def add_direct(add):
        @pl.loop(NZ, NK)
        def _(k):
            add(k)

    def forward():
        @pl.loop(0, E)
        def _(b):
            r = rows_of(b, CAP)
            pre_gate = acc_gu[r, 0:H]
            hid[r, mine_g] = (pre_gate * jax.nn.sigmoid(pre_gate) * acc_gu[r, H : 2 * H]).astype(BF16)

    def backward():
        @pl.loop(0, E)
        def _(b):
            r = rows_of(b, CAP)
            pre_gate = acc_gu[r, 0:H]
            grad_hidden = acc_h[r, :]
            sigma = jax.nn.sigmoid(pre_gate)
            gpre[r, mine_g] = (
                grad_hidden * acc_gu[r, H : 2 * H] * sigma * (1.0 + pre_gate * (1.0 - sigma))
            ).astype(BF16)
            gpre[r, mine_u] = (grad_hidden * (pre_gate * sigma)).astype(BF16)

    def weight_grads(first, last):
        @pl.loop(first, last)
        def _(k):
            kr = rows_of(k, KS)
            g = lax.dot_general(xd[0, k], gpre[:, mine_g], TN, preferred_element_type=F32)
            gg[kr, :] = g.astype(BF16)
            u = lax.dot_general(xd[0, k], gpre[:, mine_u], TN, preferred_element_type=F32)
            gu[kr, :] = u.astype(BF16)
            w = lax.dot_general(hid[:, mine_g], xd[1, k], TN, preferred_element_type=F32)
            gd[:, kr] = w.astype(BF16)

    def program(t):
        pending = []

        def send(src, dst, ss, rs, device):
            c = remote(src, dst, ss, rs, device)
            c.start()
            pending.append(c)

        if t == 1:
            slot_weight = jnp.sum(spread0 * w0_row + spread1 * w1_row, axis=1, keepdims=True)

        def dispatch(cols):
            v = jnp.dot(spread, cols, preferred_element_type=F32)
            return (v if t == 0 else slot_weight * v).astype(BF16)

        def exchange_slice():
            for i in range(1, E):
                j = lax.rem(e + i, E)
                send(
                    send_s.at[rows_of(j, CAP), :], xd.at[t, z, own_rows, :],
                    a_send.at[i - 1], a_recv.at[i - 1], dev(j, yh, z, core),
                )

        def slice_arrived():
            for i in range(1, E):
                src = rows_of(lax.rem(e + E - i, E), CAP)
                arrived(xd.at[t, z, src, :], a_send.at[i - 1], a_recv.at[i - 1])

        def exchange_direct():
            for i in range(1, E):
                j = lax.rem(e + i, E)
                send(
                    send_d.at[:, rows_of(j, CAP), :], xd.at[t, NZ:NK, own_rows, :],
                    d_send.at[i - 1], d_recv.at[i - 1], dev(j, yh, z, core),
                )

        def direct_arrived():
            for i in range(1, E):
                src = rows_of(lax.rem(e + E - i, E), CAP)
                arrived(xd.at[t, NZ:NK, src, :], d_send.at[i - 1], d_recv.at[i - 1])
            send(xd.at[t, NZ:NK], xd.at[t, NZ:NK], dsib_sem.at[0], dsib_sem.at[1], sibling)

        def gather(view, parts, sems):
            s_send, s_recv, b_send, b_recv = sems

            for s in range(5):
                for p in range(parts):
                    for way, nxt, sign in ((0, up, -1), (1, down, 1)):
                        split = (p < parts // 2) == (way == 0)
                        if s == 4 and not split:
                            continue
                        ref = view(t, zmod(z + sign * s), p)
                        if s > 0:
                            arrived(ref, s_send.at[way, s - 1, p], s_recv.at[way, s - 1, p])
                        if s < 3 or (s == 3 and split):
                            send(ref, ref, s_send.at[way, s, p], s_recv.at[way, s, p], nxt)
                        if s > 0 or way == 0:
                            d = (sign * s) % NZ
                            send(ref, ref, b_send.at[d, p], b_recv.at[d, p], sibling)
                yield

        def scatter(view, sems):
            s_send, s_recv, b_send, b_recv = sems
            ref = view(t, z)
            for dz in (4, 3, 5, 2, 6, 1, 7):
                to = dev(e, yh, lax.rem(z + dz, NZ), core)
                send(ref, ref, s_send.at[dz // 4, dz % 4, 0], s_recv.at[dz // 4, dz % 4, 0], to)
            send(ref, ref, b_send.at[0, 0], b_recv.at[0, 0], sibling)
            yield
            for dz in (1, 7, 2, 6, 3, 5, 4):
                ref = view(t, zmod(z - dz))
                arrived(ref, s_send.at[dz // 4, dz % 4, 0], s_recv.at[dz // 4, dz % 4, 0])
                send(ref, ref, b_send.at[NZ - dz, 0], b_recv.at[NZ - dz, 0], sibling)
            yield

        def term(zd):
            cols = rows_of(zd, RS)
            if t == 0:
                v = jnp.dot(hid[...], wd[:, cols], preferred_element_type=F32)
            else:
                v = lax.dot_general(gpre[...], wgu[cols, :], NT, preferred_element_type=F32)
            for q in range(NQ):
                part[q, zd] = v[:, q * QC : (q + 1) * QC].astype(BF16)

        def other_terms():
            @pl.loop(0, 5)
            def _(i):
                term(zmod(z + 6 + i))

        probs = []

        def back(q):
            def rs_start(way, s, h):
                send(
                    part.at[q, target(way, s), half(h), :], land[way].at[q, s, half(h), :],
                    rs_send.at[q, way * 4 + s, h], rs_recv.at[q, way * 4 + s, h], up if way == 0 else down,
                )

            def rs_arrived(way, s, h):
                arrived(land[way].at[q, s, half(h), :], rs_send.at[q, way * 4 + s, h], rs_recv.at[q, way * 4 + s, h])

            def rs_add(way, s, h):
                zd = target(way, s + 1)
                part[q, zd, half(h), :] = (
                    part[q, zd, half(h), :].astype(F32) + land[way][q, s, half(h), :].astype(F32)
                ).astype(BF16)

            if q == 0:
                term(zmod(z + 4))
            rs_start(0, 0, 0)
            rs_start(1, 0, 1)
            if q == 0:
                term(zmod(z + 3))
            rs_start(0, 1, 1)
            if q == 0:
                term(zmod(z + 5))
            rs_start(1, 1, 0)
            yield
            for way, h in ((0, 0), (1, 1)):
                rs_arrived(way, 0, h)
                rs_add(way, 0, h)
                rs_start(way, 1, h)
            yield
            for s in (1, 2):
                for way, h in ((0, 1), (1, 0), (0, 0), (1, 1)):
                    rs_arrived(way, s, h)
                    rs_add(way, s, h)
                    rs_start(way, s + 1, h)
                yield
            for h in range(2):
                for way in range(2):
                    rs_arrived(way, 3, h)
                part[q, z, half(h), :] = (
                    part[q, z, half(h), :].astype(F32)
                    + rp[q, 3, half(h), :].astype(F32)
                    + rm[q, 3, half(h), :].astype(F32)
                ).astype(BF16)
            rc[q, yh, own_rows, :] = part[q, z, own_rows, :]
            for i in range(E):
                for dy in range(2):
                    if i or dy:
                        b = lax.rem(e + i, E)
                        send(
                            part.at[q, z, rows_of(b, CAP), :], rc.at[q, yh, own_rows, :],
                            c_send.at[q, i * 2 + dy], c_recv.at[q, i * 2 + dy],
                            dev(b, lax.rem(yh + dy, 2), z, core),
                        )
            yield
            for i in range(E):
                for dy in range(2):
                    if i or dy:
                        src = rows_of(lax.rem(e + E - i, E), CAP)
                        arrived(
                            rc.at[q, lax.rem(yh + dy, 2), src, :],
                            c_send.at[q, i * 2 + dy], c_recv.at[q, i * 2 + dy],
                        )
            summed = (rc[q, 0].astype(F32) + rc[q, 1].astype(F32)).astype(BF16)
            out0 = jnp.dot(pick0, summed, preferred_element_type=F32)
            out1 = jnp.dot(pick1, summed, preferred_element_type=F32)
            mixed = w0 * out0 + w1 * out1 if t == 0 else out0 + out1
            outs[t, :, pl.ds(pl.multiple_of(z * RS + q * QC, QC), QC)] = mixed.astype(BF16)

            def columns(zz):
                return pl.ds(pl.multiple_of(zz * RS + q * QC, QC), QC)

            def half_view(kind, zz, p):
                return outs.at[kind, p * (TOK // 2) : (p + 1) * (TOK // 2), columns(zz)]

            def whole_view(kind, zz, p=0):
                return outs.at[kind, :, columns(zz)]

            sems = (o_send.at[q], o_recv.at[q], osib_send.at[q], osib_recv.at[q])
            straight = q >= NQ - 1 - t
            steps = scatter(whole_view, sems) if straight else gather(half_view, 2, sems)
            next(steps)
            if t == 0:
                cot = cot_part[:, q * QC : (q + 1) * QC].astype(F32)
                probs.append((jnp.sum(cot * out0, axis=1, keepdims=True), jnp.sum(cot * out1, axis=1, keepdims=True)))
                if q == NQ - 1:
                    p0 = sum(v[0] for v in probs)
                    p1 = sum(v[1] for v in probs)
                    gp[z] = (jnp.where(lane == 0, p0, 0.0) + jnp.where(lane == 1, p1, 0.0)).T[0:8, :]
                    for dz in range(1, NZ):
                        send(gp.at[z], gp.at[z], g_send.at[dz], g_recv.at[dz], dev(e, yh, lax.rem(z + dz, NZ), core))
            yield
            for _ in steps:
                yield
            for d in range(NZ):
                if q >= NQ - 2 + t:
                    sib_arrived(whole_view, 1 - t, 1, sems, d)
                else:
                    sib_arrived(half_view, 1 - t, 2, sems, d)
            yield

        loads[t][0].wait()
        send_s[...] = dispatch(acts_s[...])
        xd[t, z, own_rows, :] = send_s[own_rows, :]
        pl.semaphore_wait(barrier, 2 * E - 1 + NZ)
        if t == 0:
            exchange_slice()
            send(w_gate.at[0], wgu.at[:, 0:H], wpre_sem.at[0], wpre_sem.at[2], sibling)
            send(w_up.at[0], wgu.at[:, 2 * H : 3 * H], wpre_sem.at[1], wpre_sem.at[3], sibling)
        else:
            send(w_down.at[0], wd.at[H : 2 * H, :], wpre_sem.at[0], wpre_sem.at[2], sibling)
        loads[t][1].wait()
        for k in range(ND):
            send_d[k] = dispatch(acts_d[:, k * KS : (k + 1) * KS])
        for k in range(ND):
            xd[t, NZ + k, own_rows, :] = send_d[k, own_rows, :]
        acc_gu[...] = jnp.zeros_like(acc_gu)
        acc_h[...] = jnp.zeros_like(acc_h)
        pick0 = spread0.T.astype(BF16)
        pick1 = spread1.T.astype(BF16)
        if t == 0:
            w0 = jnp.broadcast_to(w0_row, (TOK, TOK)).T[:, 0:1]
            w1 = jnp.broadcast_to(w1_row, (TOK, TOK)).T[:, 0:1]
        for c in (own_g, own_u, own_d, own_c):
            c.wait()
        ring = gather(xd_view, NP, ring_sems)
        q0, q1, q2 = (back(q) for q in range(NQ))

        def go(*order):
            for q in order:
                next(q)

        def sib_slices(*ds):
            for d in ds:
                sib_arrived(xd_view, 1 - t, NP, ring_sems, d)

        if t == 0:
            slice_arrived()
            go(ring)
            exchange_direct()
            add_x(z)
            go(ring)
            add_pair(add_x, 1)
            go(ring)
            add_pair(add_x, 2)
            go(ring)
            add_pair(add_x, 3)
            direct_arrived()
            add_direct(add_x)
            go(ring)
            add_x(zmod(z + 4))
            forward()
            arrived(wd.at[H : 2 * H, :], wpre_sem.at[0], wpre_sem.at[2])
            arrived(hid.at[:, H : 2 * H], act_sem.at[0], act_sem.at[2])
            go(q0, q1)
            other_terms()
            go(q2)
            sib_slices(0, 1, -1)
            add_y(z)
            add_pair(add_y, 1)
            go(q0)
            sib_slices(2, -2)
            add_pair(add_y, 2)
            go(q1)
            sib_slices(3, -3)
            add_pair(add_y, 3)
            arrived(xd.at[1, NZ:NK], dsib_sem.at[0], dsib_sem.at[1])
            add_direct(add_y)
            go(q2)
            sib_slices(4)
            add_y(zmod(z + 4))
            backward()
            send(gpre.at[:, 0:H], gpre.at[:, 0:H], act_sem.at[0], act_sem.at[2], sibling)
            send(gpre.at[:, 2 * H : 3 * H], gpre.at[:, 2 * H : 3 * H], act_sem.at[1], act_sem.at[3], sibling)
            go(q0, q1, q2)
            weight_grads(0, 4)
            go(q0, q1, q2)
            weight_grads(4, 8)
            go(q0, q1, q2)
            weight_grads(8, 12)
            go(q0, q1, q2, q0, q1, q0, q1, q2, q0, q1, q0, q1)
            for dz in range(1, NZ):
                arrived(gp.at[zmod(z - dz)], g_send.at[dz], g_recv.at[dz])
            total = gp[0]
            for zz in range(1, NZ):
                total = total + gp[zz]
            gp_sum[...] = total
            send(gp_sum, gp_sum, gsum_sem.at[0], gsum_sem.at[1], sibling)
            go(q0, q1, q2)
        else:
            sib_slices(0)
            exchange_slice()
            add_x(z)
            sib_slices(1, -1)
            add_pair(add_x, 1)
            slice_arrived()
            sib_slices(2, -2)
            add_pair(add_x, 2)
            sib_slices(3, -3)
            go(ring)
            exchange_direct()
            add_pair(add_x, 3)
            arrived(xd.at[0, NZ:NK], dsib_sem.at[0], dsib_sem.at[1])
            add_direct(add_x)
            sib_slices(4)
            add_x(zmod(z + 4))
            forward()
            send(hid.at[:, H : 2 * H], hid.at[:, H : 2 * H], act_sem.at[0], act_sem.at[2], sibling)
            go(ring)
            add_y(z)
            add_pair(add_y, 1)
            go(ring)
            add_pair(add_y, 2)
            go(ring)
            add_pair(add_y, 3)
            direct_arrived()
            add_direct(add_y)
            go(ring)
            add_y(zmod(z + 4))
            backward()
            arrived(wgu.at[:, 0:H], wpre_sem.at[0], wpre_sem.at[2])
            arrived(wgu.at[:, 2 * H : 3 * H], wpre_sem.at[1], wpre_sem.at[3])
            arrived(gpre.at[:, 0:H], act_sem.at[0], act_sem.at[2])
            arrived(gpre.at[:, 2 * H : 3 * H], act_sem.at[1], act_sem.at[3])
            go(q0, q1)
            other_terms()
            go(q0, q2)
            weight_grads(0, 4)
            go(q0, q1)
            weight_grads(4, 8)
            go(q0, q1, q2)
            weight_grads(8, 12)
            go(q0, q1, q2, q2, q1, q0, q2, q1, q0, q0, q2, q0, q0, q1, q2, q0, q1, q2)
            arrived(gp_sum, gsum_sem.at[0], gsum_sem.at[1])

        for q in (ring, q0, q1, q2):
            assert next(q, None) is None
        prob[...] = gp_sum[0:2, :]
        for c in pending:
            c.wait_send()

    for c in range(2):

        @pl.when(core == c)
        def _(c=c):
            program(c)


def store(outs, prob, gg, gu, gd, moe_out, grad_tokens, grad_prob, grad_gate, grad_up, grad_down, sem):
    copies = []
    for i, (src, dst) in enumerate((
        (gg, grad_gate.at[0]), (gu, grad_up.at[0]), (gd, grad_down.at[0]),
        (outs.at[0], moe_out), (outs.at[1], grad_tokens), (prob, grad_prob),
    )):
        copies.append(pltpu.make_async_copy(src, dst, sem.at[i]))
    for c in copies:
        c.start()
    for c in copies:
        c.wait()


def per_device(tokens, assignment, route_weight, cotangent, w_gate, w_up, w_down):
    hbm = pl.BlockSpec(memory_space=pl.ANY)
    vmem = pl.BlockSpec(memory_space=pltpu.VMEM)
    dma = pltpu.SemaphoreType.DMA
    held = pl.pallas_call(
        kernel,
        out_shape=(
            pltpu.VMEM((2, TOK, D), BF16),
            pltpu.VMEM((2, TOK), F32),
            pltpu.VMEM((D, H), BF16),
            pltpu.VMEM((D, H), BF16),
            pltpu.VMEM((H, D), BF16),
        ),
        in_specs=[hbm, vmem, vmem, hbm, hbm, hbm, hbm],
        out_specs=(vmem,) * 5,
        scratch_shapes=[
            pltpu.VMEM((TOK, KS), BF16),
            pltpu.VMEM((TOK, ND * KS), BF16),
            pltpu.VMEM((TOK, RS), BF16),
            pltpu.VMEM((D, 4 * H), BF16),
            pltpu.VMEM((2 * H, D), BF16),
            pltpu.VMEM((SLOTS, KS), BF16),
            pltpu.VMEM((ND, SLOTS, KS), BF16),
            pltpu.VMEM((2, NK, SLOTS, KS), BF16),
            pltpu.VMEM((SLOTS, 2 * H), F32),
            pltpu.VMEM((SLOTS, H), F32),
            pltpu.VMEM((SLOTS, 2 * H), BF16),
            pltpu.VMEM((SLOTS, 4 * H), BF16),
            pltpu.VMEM((NQ, NZ, SLOTS, QC), BF16),
            pltpu.VMEM((NQ, 4, SLOTS, QC), BF16),
            pltpu.VMEM((NQ, 4, SLOTS, QC), BF16),
            pltpu.VMEM((NQ, 2, SLOTS, QC), BF16),
            pltpu.VMEM((NZ, 8, TOK), F32),
            pltpu.VMEM((8, TOK), F32),
            dma((6,)), dma((4,)),
            dma((E - 1,)), dma((E - 1,)), dma((E - 1,)), dma((E - 1,)),
            dma((2, 4, NP)), dma((2, 4, NP)), dma((NZ, NP)), dma((NZ, NP)), dma((2,)),
            dma((4,)), dma((NQ, 8, 2)), dma((NQ, 8, 2)), dma((NQ, 2 * E)), dma((NQ, 2 * E)),
            dma((NQ, 2, 4, 2)), dma((NQ, 2, 4, 2)), dma((NQ, NZ, 2)), dma((NQ, NZ, 2)),
            dma((NZ,)), dma((NZ,)), dma((2,)),
        ],
        compiler_params=pltpu.CompilerParams(
            collective_id=0, has_side_effects=True, vmem_limit_bytes=50 * 1024 * 1024
        ),
    )(tokens, assignment.T, route_weight.T, cotangent, w_gate, w_up, w_down)
    moe_out, grad_tokens, grad_prob, grad_gate, grad_up, grad_down = pl.pallas_call(
        store,
        out_shape=(
            jax.ShapeDtypeStruct((TOK, D), BF16),
            jax.ShapeDtypeStruct((TOK, D), BF16),
            jax.ShapeDtypeStruct((2, TOK), F32),
            jax.ShapeDtypeStruct((1, D, H), BF16),
            jax.ShapeDtypeStruct((1, D, H), BF16),
            jax.ShapeDtypeStruct((1, H, D), BF16),
        ),
        in_specs=[vmem] * 5,
        out_specs=(hbm,) * 6,
        scratch_shapes=[dma((6,))],
        compiler_params=pltpu.CompilerParams(vmem_limit_bytes=16 * 1024 * 1024),
    )(*held)
    return (moe_out, grad_tokens, grad_prob.T, grad_gate, grad_up, grad_down)


def solution(mesh):
    return jax.shard_map(
        per_device,
        mesh=mesh,
        in_specs=(
            P("expert", None),
            P("expert", None),
            P("expert", None),
            P("expert", None),
            P("expert", None, "fsdp"),
            P("expert", None, "fsdp"),
            P("expert", "fsdp", None),
        ),
        out_specs=(
            P("expert", None),
            P("expert", None),
            P("expert", None),
            P("expert", None, "fsdp"),
            P("expert", None, "fsdp"),
            P("expert", "fsdp", None),
        ),
        check_vma=False,
    )
```

time: 468 us -> 96.5 us (0.21); the launches traced: 462 us -> 96.4 us
  waiting for transfers between devices: 207 us -> 0 us
  Pallas kernels: 0 us -> 95.6 us
  starting transfers between devices: 84.5 us -> 0 us
  blocking collectives: 83.1 us -> 0 us
  matrix products: 44.1 us -> 0 us
  local copies, waits for them, and re-layouts: 25.5 us -> 0 us
  between operations: 15.1 us -> 0.8 us
    all_gather x2 -> x0, waiting for transfers between devices: 125 us -> none  [return_rows(): summed = lax.all_gather(shares, 'fsdp', axis=0, tiled=True)]
    pallas_call x0 -> x2, Pallas kernels: none -> 95.6 us  [the longest x1 92.9 us: per_device(): pl.pallas_call(kernel, out_shape=(pltpu.VMEM((2, TOK, D), BF16), pltpu.VM...]
    unnamed x1 -> x0, blocking collectives: 83.1 us -> none
    unnamed x16 -> x0, starting transfers between devices: 65.1 us -> none
    all_to_all x4 -> x0, waiting for transfers between devices: 64.9 us -> none  [the longest x2 49.5 us: spread(): lax.all_to_all(blocks, 'expert', split_axis=0, concat_axis=0, tiled=True)]
    dot_general x16 -> x0, matrix products: 44.1 us -> none  [the longest x1 3.87 us: per_device(): jnp.dot(gathered.T, grad_pre_gate, preferred_element_type=jnp.float32)]
    all_to_all x4 -> x0, starting transfers between devices: 19.3 us -> none  [the longest x2 10.4 us: spread(): lax.all_to_all(blocks, 'expert', split_axis=0, concat_axis=0, tiled=True)]
    unnamed x18 -> x0, waiting for transfers between devices: 17.2 us -> none
  transfers between devices with their start and end apart: 22 -> 0, of which waited for: 10 -> 0; matrix products, arithmetic and copies ran while one was open for 9% -> 0% of each run, Pallas kernels for 0% -> 0%
where the time goes in v3:
time: 96.5 us; the launch traced here: 96.4 us
  Pallas kernels  95.6 us (99%)
    pallas_call x1, Pallas kernels, per_device(): pl.pallas_call(kernel, out_shape=(pltpu.VMEM((2, TOK, D), BF16), pltpu.VM...  92.9 us
    pallas_call x1, Pallas kernels, per_device(): pl.pallas_call(store, out_shape=(jax.ShapeDtypeStruct((TOK, D), BF16), ja...  2.73 us

profile of v3, /device:TPU:1, one launch (start us, length us, event | category | flops | bytes accessed | tf_op | source)
XLA Modules:
  0.0 96.4 jit_solution(17619320273656505501)
XLA Ops:
  0.6 92.9 %shard_map.118 = (bf16[2,128,3072]{2,1,0:T(8,128)(2,1)S(1)}, f32[2,128]{1,0:T(2,128)S(1)}, bf16[3072,256]{1,0:T(8,128)(2,1)S(1)}, bf16[3072,256]{1,0:T(8,128)(2,1)S(1)}, bf16[256,3072]{1,0:T(8,128)(2,1)S(1)}) custom-call(bf16[128,3072]{1,0:T(8,128)(2,1)} %tokens.1, s32[2,128]{1,0:T(2,128)} %bitcast.3, f32[2,128]{1,0:T(2,128)} %bitcast.4, ...), custom_call_target="tpu_custom_call" | custom-call | tf_op jit(solution)/shard_map/pallas_call | solution.py:543
  93.5 2.7 %shard_map.119 = (bf16[128,3072]{1,0:T(8,128)(2,1)}, bf16[128,3072]{1,0:T(8,128)(2,1)}, f32[2,128]{1,0:T(2,128)}, bf16[1,3072,256]{2,1,0:T(8,128)(2,1)}, bf16[1,...) custom-call(bf16[2,128,3072]{2,1,0:T(8,128)(2,1)S(1)} %get-tuple-element.17.outs, ...), custom_call_target="tpu_custom_call" | custom-call | tf_op jit(solution)/shard_map/pallas_call | solution.py:584

commit v4 on v3

v4 whole, which is shorter than its diff:
```python
import jax
import jax.numpy as jnp
from jax import lax
from jax.experimental import pallas as pl
from jax.experimental.pallas import tpu as pltpu
from jax.sharding import PartitionSpec as P

MESH = pl.DeviceIdType.MESH
BF16 = jnp.bfloat16
F32 = jnp.float32
NT = (((1,), (1,)), ((), ()))
TN = (((0,), (0,)), ((), ()))

E = 8
NZ = 8
CAP = 48
TOK = 128
SLOTS = E * CAP
D = 3072
H = 256
HALF = SLOTS // 2
NG = 4
KG = D // NG
RS = D // NZ
QC = 128
NQ = RS // QC
NP = 4


def rows_of(index, size):
    return pl.ds(pl.multiple_of(index * size, size), size)


def kernel(
    tokens, assign_t, weight_t, cotangent, w_gate, w_up, w_down,
    outs, prob, gg, gu, gd,
    acts, cot_part, wgu, wd, send_x, send_y, xg, yd, acc_gu, acc_h, hid, gpre,
    part, rp, rm, rc, gp, gp_sum,
    load_sem, wpre_sem,
    a_send, a_recv, d_send, d_recv, ring_send, ring_recv, sib_send, sib_recv, dsib_send, dsib_recv,
    act_sem, rs_send, rs_recv, c_send, c_recv, o_send, o_recv, osib_send, osib_recv, g_send, g_recv, gsum_sem,
):
    e = lax.axis_index("expert")
    f = lax.axis_index("fsdp")
    core = lax.rem(f, 2)
    z = lax.rem(lax.div(f, 2), NZ)
    yh = lax.div(f, 2 * NZ)

    def dev(e_, yh_, z_, c_):
        return (e_, yh_ * (2 * NZ) + z_ * 2 + c_)

    sibling = dev(e, yh, z, 1 - core)
    up = dev(e, yh, lax.rem(z + 1, NZ), core)
    down = dev(e, yh, lax.rem(z + NZ - 1, NZ), core)

    def zmod(v):
        return lax.rem(v + 2 * NZ, NZ)

    def remote(src, dst, ss, rs, device):
        return pltpu.make_async_remote_copy(
            src_ref=src, dst_ref=dst, send_sem=ss, recv_sem=rs, device_id=device, device_id_type=MESH
        )

    def arrived(dst, ss, rs):
        remote(dst, dst, ss, rs, sibling).wait_recv()

    load_x = [
        pltpu.make_async_copy(tokens.at[:, g * KG : (g + 1) * KG], acts.at[g], load_sem.at[5 + g]) for g in range(NG)
    ]
    own_c = pltpu.make_async_copy(cotangent.at[:, rows_of(z, RS)], cot_part, load_sem.at[4])
    own_c.start()

    @pl.when(core == 0)
    def _():
        for c in load_x:
            c.start()

    own_g = pltpu.make_async_copy(w_gate.at[0], wgu.at[:, rows_of(core, H)], load_sem.at[1])
    own_u = pltpu.make_async_copy(w_up.at[0], wgu.at[:, rows_of(core + 2, H)], load_sem.at[2])
    own_d = pltpu.make_async_copy(w_down.at[0], wd.at[rows_of(core, H), :], load_sem.at[3])
    for c in (own_g, own_u, own_d):
        c.start()

    barrier = pltpu.get_barrier_semaphore()

    def greet(device):
        pl.semaphore_signal(barrier, inc=1, device_id=device, device_id_type=MESH)

    greet(sibling)
    for i in range(E):
        for dy in range(2):
            if i or dy:
                greet(dev(lax.rem(e + i, E), lax.rem(yh + dy, 2), z, core))
    for dz in range(1, NZ):
        greet(dev(e, yh, lax.rem(z + dz, NZ), core))

    a0 = assign_t[0:1, :]
    a1 = assign_t[1:2, :]
    w0_row = weight_t[0:1, :]
    w1_row = weight_t[1:2, :]
    expert = lax.broadcasted_iota(jnp.int32, (8, TOK), 0)
    hot0 = (expert == a0).astype(F32)
    hot1 = (expert == a1).astype(F32)
    lane = lax.broadcasted_iota(jnp.int32, (TOK, TOK), 1)
    row = lax.broadcasted_iota(jnp.int32, (TOK, TOK), 0)
    before = (row < lane).astype(BF16)
    count = jnp.dot((hot0 + hot1).astype(BF16), before, preferred_element_type=F32)
    slot0 = a0 * CAP + jnp.sum(hot0 * count, axis=0, keepdims=True).astype(jnp.int32)
    slot1 = a1 * CAP + jnp.sum(hot1 * count, axis=0, keepdims=True).astype(jnp.int32)
    slot = lax.broadcasted_iota(jnp.int32, (SLOTS, TOK), 0)
    spread0 = (slot == slot0).astype(F32)
    spread1 = (slot == slot1).astype(F32)
    spread = (spread0 + spread1).astype(BF16)
    own_rows = rows_of(e, CAP)
    mine_g = rows_of(core, H)
    mine_u = rows_of(core + 2, H)
    land = (rp, rm)

    def half(h):
        return slice(h * HALF, (h + 1) * HALF)

    def target(way, s):
        return zmod(z + 4 - s) if way == 0 else zmod(z - 4 + s)

    def yd_view(zz, p):
        return yd.at[zz, p * (SLOTS // NP) : (p + 1) * (SLOTS // NP), :]

    partners = ((1, 0), (3, 0), (0, 1), (2, 0), (1, 1), (3, 1), (2, 1))
    ey = lax.div(e, 4)
    ex = lax.rem(e, 4)

    def group_of(dx, dy):
        return lax.rem(ey + dy, 2) * 4 + lax.rem(ex + dx, 4)

    def add_x(g):
        kr = rows_of(g, KG)
        acc_gu[:, 0:H] += jnp.dot(xg[g], wgu[kr, mine_g], preferred_element_type=F32)
        acc_gu[:, H : 2 * H] += jnp.dot(xg[g], wgu[kr, mine_u], preferred_element_type=F32)

    def add_y(k):
        acc_h[...] += lax.dot_general(yd[k], wd[mine_g, rows_of(k, RS)], NT, preferred_element_type=F32)

    def add_pair(s):
        @pl.loop(0, 2)
        def _(i):
            add_y(zmod(z - s + 2 * s * i))

    def forward():
        @pl.loop(0, E)
        def _(b):
            r = rows_of(b, CAP)
            pre_gate = acc_gu[r, 0:H]
            hid[r, mine_g] = (pre_gate * jax.nn.sigmoid(pre_gate) * acc_gu[r, H : 2 * H]).astype(BF16)

    def backward():
        @pl.loop(0, E)
        def _(b):
            r = rows_of(b, CAP)
            pre_gate = acc_gu[r, 0:H]
            grad_hidden = acc_h[r, :]
            sigma = jax.nn.sigmoid(pre_gate)
            gpre[r, mine_g] = (
                grad_hidden * acc_gu[r, H : 2 * H] * sigma * (1.0 + pre_gate * (1.0 - sigma))
            ).astype(BF16)
            gpre[r, mine_u] = (grad_hidden * (pre_gate * sigma)).astype(BF16)

    def weight_grads(g):
        @pl.loop(3 * g, 3 * g + 3)
        def _(k):
            kr = rows_of(k, H)
            x = xg[g, :, pl.ds(pl.multiple_of((k - 3 * g) * H, H), H)]
            gg[kr, :] = lax.dot_general(x, gpre[:, mine_g], TN, preferred_element_type=F32).astype(BF16)
            gu[kr, :] = lax.dot_general(x, gpre[:, mine_u], TN, preferred_element_type=F32).astype(BF16)

        @pl.loop(2 * g, 2 * g + 2)
        def _(k):
            w = lax.dot_general(hid[:, mine_g], yd[k], TN, preferred_element_type=F32)
            gd[:, rows_of(k, RS)] = w.astype(BF16)

    def program(t):
        pending = []

        def send(src, dst, ss, rs, device):
            c = remote(src, dst, ss, rs, device)
            c.start()
            pending.append(c)

        if t == 1:
            slot_weight = jnp.sum(spread0 * w0_row + spread1 * w1_row, axis=1, keepdims=True)

        def dispatch(cols):
            v = jnp.dot(spread, cols, preferred_element_type=F32)
            return (v if t == 0 else slot_weight * v).astype(BF16)

        def exchange_x(g):
            if g:
                send_x[g] = dispatch(acts[g])
            xg[g, own_rows, :] = send_x[g, own_rows, :]
            for i, (dx, dy) in enumerate(partners):
                j = group_of(dx, dy)
                send(
                    send_x.at[g, rows_of(j, CAP), :], xg.at[g, own_rows, :],
                    d_send.at[g, i], d_recv.at[g, i], dev(j, yh, z, core),
                )

        def x_arrived(g):
            for i, (dx, dy) in enumerate(partners):
                src = rows_of(group_of(4 - dx, dy), CAP)
                arrived(xg.at[g, src, :], d_send.at[g, i], d_recv.at[g, i])
            send(xg.at[g], xg.at[g], dsib_send.at[g], dsib_recv.at[g], sibling)

        def sib_x(g):
            arrived(xg.at[g], dsib_send.at[g], dsib_recv.at[g])

        def exchange_y():
            for i, (dx, dy) in enumerate(partners):
                j = group_of(dx, dy)
                send(
                    send_y.at[rows_of(j, CAP), :], yd.at[z, own_rows, :],
                    a_send.at[i], a_recv.at[i], dev(j, yh, z, core),
                )

        def y_arrived():
            for i, (dx, dy) in enumerate(partners):
                src = rows_of(group_of(4 - dx, dy), CAP)
                arrived(yd.at[z, src, :], a_send.at[i], a_recv.at[i])

        def sib_y(*ds):
            for d in ds:
                for p in range(NP):
                    arrived(yd_view(zmod(z + d), p), sib_send.at[d % NZ, p], sib_recv.at[d % NZ, p])

        def gather():
            for s in range(5):
                for p in range(NP):
                    for way, nxt, sign in ((0, up, -1), (1, down, 1)):
                        split = (p < NP // 2) == (way == 0)
                        if s == 4 and not split:
                            continue
                        ref = yd_view(zmod(z + sign * s), p)
                        if s > 0:
                            arrived(ref, ring_send.at[way, s - 1, p], ring_recv.at[way, s - 1, p])
                        if s < 3 or (s == 3 and split):
                            send(ref, ref, ring_send.at[way, s, p], ring_recv.at[way, s, p], nxt)
                        if s > 0 or way == 0:
                            d = (sign * s) % NZ
                            send(ref, ref, sib_send.at[d, p], sib_recv.at[d, p], sibling)
                yield

        def spread_out(view, sems):
            s_send, s_recv, b_send, b_recv = sems

            def at(dz):
                return dev(e, yh, zmod(z + dz), core)

            def pass_on(d, h=None):
                ref = view(t, zmod(z + d), h)
                k = d % NZ if h != 1 else NZ
                send(ref, ref, b_send.at[k], b_recv.at[k], sibling)

            def got(i, d, h=None):
                arrived(view(t, zmod(z + d), h), s_send.at[i], s_recv.at[i])

            def give(i, d, dz, h=None):
                ref = view(t, zmod(z + d), h)
                send(ref, ref, s_send.at[i], s_recv.at[i], at(dz))

            give(0, 0, 2)
            give(1, 0, -2)
            give(2, 0, 1)
            give(3, 0, -1)
            pass_on(0)
            yield
            got(0, -2)
            give(4, -2, 1)
            give(5, -2, 2, 0)
            got(1, 2)
            give(6, 2, -1)
            give(7, 2, -2, 1)
            pass_on(-2)
            pass_on(2)
            got(2, -1)
            pass_on(-1)
            got(3, 1)
            pass_on(1)
            yield
            got(4, -3)
            pass_on(-3)
            got(6, 3)
            pass_on(3)
            got(5, -4, 0)
            pass_on(4, 0)
            got(7, 4, 1)
            pass_on(4, 1)
            yield

        def term(zd):
            cols = rows_of(zd, RS)
            if t == 0:
                v = jnp.dot(hid[...], wd[:, cols], preferred_element_type=F32)
            else:
                v = lax.dot_general(gpre[...], wgu[cols, :], NT, preferred_element_type=F32)
            for q in range(NQ):
                part[q, zd] = v[:, q * QC : (q + 1) * QC].astype(BF16)

        def other_terms():
            @pl.loop(0, 5)
            def _(i):
                term(zmod(z + 6 + i))

        probs = []

        def back(q):
            def rs_start(way, s, h):
                send(
                    part.at[q, target(way, s), half(h), :], land[way].at[q, s, half(h), :],
                    rs_send.at[q, way * 4 + s, h], rs_recv.at[q, way * 4 + s, h], up if way == 0 else down,
                )

            def rs_arrived(way, s, h):
                arrived(land[way].at[q, s, half(h), :], rs_send.at[q, way * 4 + s, h], rs_recv.at[q, way * 4 + s, h])

            def rs_add(way, s, h):
                zd = target(way, s + 1)
                part[q, zd, half(h), :] = (
                    part[q, zd, half(h), :].astype(F32) + land[way][q, s, half(h), :].astype(F32)
                ).astype(BF16)

            if q == 0:
                term(zmod(z + 4))
            rs_start(0, 0, 0)
            rs_start(1, 0, 1)
            if q == 0:
                term(zmod(z + 3))
            rs_start(0, 1, 1)
            if q == 0:
                term(zmod(z + 5))
            rs_start(1, 1, 0)
            yield
            for way, h in ((0, 0), (1, 1)):
                rs_arrived(way, 0, h)
                rs_add(way, 0, h)
                rs_start(way, 1, h)
            yield
            for s in (1, 2):
                for way, h in ((0, 1), (1, 0), (0, 0), (1, 1)):
                    rs_arrived(way, s, h)
                    rs_add(way, s, h)
                    rs_start(way, s + 1, h)
                yield
            for h in range(2):
                for way in range(2):
                    rs_arrived(way, 3, h)
                part[q, z, half(h), :] = (
                    part[q, z, half(h), :].astype(F32)
                    + rp[q, 3, half(h), :].astype(F32)
                    + rm[q, 3, half(h), :].astype(F32)
                ).astype(BF16)
            rc[q, yh, own_rows, :] = part[q, z, own_rows, :]
            for i in range(E):
                for dy in range(2):
                    if i or dy:
                        b = lax.rem(e + i, E)
                        send(
                            part.at[q, z, rows_of(b, CAP), :], rc.at[q, yh, own_rows, :],
                            c_send.at[q, i * 2 + dy], c_recv.at[q, i * 2 + dy],
                            dev(b, lax.rem(yh + dy, 2), z, core),
                        )
            yield
            for i in range(E):
                for dy in range(2):
                    if i or dy:
                        src = rows_of(lax.rem(e + E - i, E), CAP)
                        arrived(
                            rc.at[q, lax.rem(yh + dy, 2), src, :],
                            c_send.at[q, i * 2 + dy], c_recv.at[q, i * 2 + dy],
                        )
            summed = (rc[q, 0].astype(F32) + rc[q, 1].astype(F32)).astype(BF16)
            out0 = jnp.dot(pick0, summed, preferred_element_type=F32)
            out1 = jnp.dot(pick1, summed, preferred_element_type=F32)
            mixed = w0 * out0 + w1 * out1 if t == 0 else out0 + out1
            outs[t, q, z] = mixed.astype(BF16)

            def view(kind, zz, h=None):
                rows = slice(0, TOK) if h is None else slice(h * (TOK // 2), (h + 1) * (TOK // 2))
                return outs.at[kind, q, zz, rows, :]

            sems = (o_send.at[q], o_recv.at[q], osib_send.at[q], osib_recv.at[q])
            steps = spread_out(view, sems)
            next(steps)
            if t == 0:
                cot = cot_part[:, q * QC : (q + 1) * QC].astype(F32)
                probs.append((jnp.sum(cot * out0, axis=1, keepdims=True), jnp.sum(cot * out1, axis=1, keepdims=True)))
                if q == NQ - 1:
                    p0 = sum(v[0] for v in probs)
                    p1 = sum(v[1] for v in probs)
                    gp[z] = (jnp.where(lane == 0, p0, 0.0) + jnp.where(lane == 1, p1, 0.0)).T[0:8, :]
                    for dz in range(1, NZ):
                        send(gp.at[z], gp.at[z], g_send.at[dz], g_recv.at[dz], dev(e, yh, lax.rem(z + dz, NZ), core))
            yield
            for _ in steps:
                yield
            for k in range(NZ + 1):
                h = None if k not in (4, NZ) else k // NZ
                arrived(view(1 - t, zmod(z + (4 if k == NZ else k)), h), osib_send.at[q, k], osib_recv.at[q, k])
            yield

        if t == 0:
            load_x[0].wait()
            send_x[0] = dispatch(acts[0])
        else:
            own_c.wait()
            send_y[...] = dispatch(cot_part[...])
            yd[z, own_rows, :] = send_y[own_rows, :]
        pl.semaphore_wait(barrier, 2 * E - 1 + NZ)
        if t == 0:
            for g in range(NG):
                if g:
                    load_x[g].wait()
                exchange_x(g)
            send(w_gate.at[0], wgu.at[:, 0:H], wpre_sem.at[0], wpre_sem.at[2], sibling)
            send(w_up.at[0], wgu.at[:, 2 * H : 3 * H], wpre_sem.at[1], wpre_sem.at[3], sibling)
        else:
            exchange_y()
            send(w_down.at[0], wd.at[H : 2 * H, :], wpre_sem.at[0], wpre_sem.at[2], sibling)
        acc_gu[...] = jnp.zeros_like(acc_gu)
        acc_h[...] = jnp.zeros_like(acc_h)
        pick0 = spread0.T.astype(BF16)
        pick1 = spread1.T.astype(BF16)
        if t == 0:
            w0 = jnp.broadcast_to(w0_row, (TOK, TOK)).T[:, 0:1]
            w1 = jnp.broadcast_to(w1_row, (TOK, TOK)).T[:, 0:1]
            own_c.wait()
        for c in (own_g, own_u, own_d):
            c.wait()
        ring = gather()
        q0, q1, q2 = (back(q) for q in range(NQ))

        def go(*order):
            for q in order:
                next(q)

        if t == 0:
            x_arrived(0)
            add_x(0)
            sib_y(0)
            add_y(z)
            x_arrived(1)
            add_x(1)
            sib_y(1, -1)
            add_pair(1)
            x_arrived(2)
            add_x(2)
            sib_y(2, -2)
            add_pair(2)
            x_arrived(3)
            add_x(3)
            forward()
            sib_y(3, -3)
            add_pair(3)
            sib_y(4)
            add_y(zmod(z + 4))
            backward()
            send(gpre.at[:, 0:H], gpre.at[:, 0:H], act_sem.at[0], act_sem.at[2], sibling)
            send(gpre.at[:, 2 * H : 3 * H], gpre.at[:, 2 * H : 3 * H], act_sem.at[1], act_sem.at[3], sibling)
            arrived(wd.at[H : 2 * H, :], wpre_sem.at[0], wpre_sem.at[2])
            arrived(hid.at[:, H : 2 * H], act_sem.at[0], act_sem.at[2])
        else:
            y_arrived()
            go(ring)
            add_y(z)
            go(ring)
            add_pair(1)
            sib_x(0)
            add_x(0)
            go(ring)
            add_pair(2)
            sib_x(1)
            add_x(1)
            go(ring)
            add_pair(3)
            sib_x(2)
            add_x(2)
            go(ring)
            add_y(zmod(z + 4))
            sib_x(3)
            add_x(3)
            forward()
            send(hid.at[:, H : 2 * H], hid.at[:, H : 2 * H], act_sem.at[0], act_sem.at[2], sibling)
            backward()
            arrived(wgu.at[:, 0:H], wpre_sem.at[0], wpre_sem.at[2])
            arrived(wgu.at[:, 2 * H : 3 * H], wpre_sem.at[1], wpre_sem.at[3])
            arrived(gpre.at[:, 0:H], act_sem.at[0], act_sem.at[2])
            arrived(gpre.at[:, 2 * H : 3 * H], act_sem.at[1], act_sem.at[3])
        go(q0, q1)
        other_terms()
        go(q0, q2)
        weight_grads(0)
        go(q0, q1)
        weight_grads(1)
        go(q0, q1, q2)
        weight_grads(2)
        go(q0, q1, q2)
        weight_grads(3)
        go(q1, q2)
        go(q0)
        go(q2)
        go(q1, q0)
        go(q0, q1)
        go(q2)
        go(q1)
        go(q2)
        go(q2)
        if t == 0:
            for dz in range(1, NZ):
                arrived(gp.at[zmod(z - dz)], g_send.at[dz], g_recv.at[dz])
            total = gp[0]
            for zz in range(1, NZ):
                total = total + gp[zz]
            gp_sum[...] = total
            send(gp_sum, gp_sum, gsum_sem.at[0], gsum_sem.at[1], sibling)
        else:
            arrived(gp_sum, gsum_sem.at[0], gsum_sem.at[1])
        go(q0, q1, q2)

        for q in (ring, q0, q1, q2):
            assert (t == 0 and q is ring) or next(q, None) is None
        prob[...] = gp_sum[0:2, :]
        for c in pending:
            c.wait_send()

    for c in range(2):

        @pl.when(core == c)
        def _(c=c):
            program(c)


def store(outs, prob, gg, gu, gd, moe_out, grad_tokens, grad_prob, grad_gate, grad_up, grad_down, sem):
    copies = []

    def copy(src, dst, i):
        c = pltpu.make_async_copy(src, dst, sem.at[i])
        c.start()
        copies.append(c)

    for kind, dst in enumerate((moe_out, grad_tokens)):
        for q in range(NQ):
            for zz in range(NZ):
                columns = slice(zz * RS + q * QC, zz * RS + (q + 1) * QC)
                copy(outs.at[kind, q, zz], dst.at[:, columns], (kind * NQ + q) * NZ + zz)
    first = 2 * NQ * NZ
    copy(gg, grad_gate.at[0], first)
    copy(gu, grad_up.at[0], first + 1)
    copy(gd, grad_down.at[0], first + 2)
    copy(prob, grad_prob, first + 3)
    for c in copies:
        c.wait()


def per_device(tokens, assignment, route_weight, cotangent, w_gate, w_up, w_down):
    hbm = pl.BlockSpec(memory_space=pl.ANY)
    vmem = pl.BlockSpec(memory_space=pltpu.VMEM)
    dma = pltpu.SemaphoreType.DMA
    held = pl.pallas_call(
        kernel,
        out_shape=(
            pltpu.VMEM((2, NQ, NZ, TOK, QC), BF16),
            pltpu.VMEM((2, TOK), F32),
            pltpu.VMEM((D, H), BF16),
            pltpu.VMEM((D, H), BF16),
            pltpu.VMEM((H, D), BF16),
        ),
        in_specs=[hbm, vmem, vmem, hbm, hbm, hbm, hbm],
        out_specs=(vmem,) * 5,
        scratch_shapes=[
            pltpu.VMEM((NG, TOK, KG), BF16),
            pltpu.VMEM((TOK, RS), BF16),
            pltpu.VMEM((D, 4 * H), BF16),
            pltpu.VMEM((2 * H, D), BF16),
            pltpu.VMEM((NG, SLOTS, KG), BF16),
            pltpu.VMEM((SLOTS, RS), BF16),
            pltpu.VMEM((NG, SLOTS, KG), BF16),
            pltpu.VMEM((NZ, SLOTS, RS), BF16),
            pltpu.VMEM((SLOTS, 2 * H), F32),
            pltpu.VMEM((SLOTS, H), F32),
            pltpu.VMEM((SLOTS, 2 * H), BF16),
            pltpu.VMEM((SLOTS, 4 * H), BF16),
            pltpu.VMEM((NQ, NZ, SLOTS, QC), BF16),
            pltpu.VMEM((NQ, 4, SLOTS, QC), BF16),
            pltpu.VMEM((NQ, 4, SLOTS, QC), BF16),
            pltpu.VMEM((NQ, 2, SLOTS, QC), BF16),
            pltpu.VMEM((NZ, 8, TOK), F32),
            pltpu.VMEM((8, TOK), F32),
            dma((5 + NG,)), dma((4,)),
            dma((E - 1,)), dma((E - 1,)), dma((NG, E - 1)), dma((NG, E - 1)),
            dma((2, 4, NP)), dma((2, 4, NP)), dma((NZ, NP)), dma((NZ, NP)), dma((NG,)), dma((NG,)),
            dma((4,)), dma((NQ, 8, 2)), dma((NQ, 8, 2)), dma((NQ, 2 * E)), dma((NQ, 2 * E)),
            dma((NQ, 8)), dma((NQ, 8)), dma((NQ, NZ + 1)), dma((NQ, NZ + 1)),
            dma((NZ,)), dma((NZ,)), dma((2,)),
        ],
        compiler_params=pltpu.CompilerParams(
            collective_id=0, has_side_effects=True, vmem_limit_bytes=50 * 1024 * 1024
        ),
    )(tokens, assignment.T, route_weight.T, cotangent, w_gate, w_up, w_down)
    moe_out, grad_tokens, grad_prob, grad_gate, grad_up, grad_down = pl.pallas_call(
        store,
        out_shape=(
            jax.ShapeDtypeStruct((TOK, D), BF16),
            jax.ShapeDtypeStruct((TOK, D), BF16),
            jax.ShapeDtypeStruct((2, TOK), F32),
            jax.ShapeDtypeStruct((1, D, H), BF16),
            jax.ShapeDtypeStruct((1, D, H), BF16),
            jax.ShapeDtypeStruct((1, H, D), BF16),
        ),
        in_specs=[vmem] * 5,
        out_specs=(hbm,) * 6,
        scratch_shapes=[dma((2 * NQ * NZ + 4,))],
        compiler_params=pltpu.CompilerParams(vmem_limit_bytes=16 * 1024 * 1024),
    )(*held)
    return (moe_out, grad_tokens, grad_prob.T, grad_gate, grad_up, grad_down)


def solution(mesh):
    return jax.shard_map(
        per_device,
        mesh=mesh,
        in_specs=(
            P("expert", None),
            P("expert", None),
            P("expert", None),
            P("expert", None),
            P("expert", None, "fsdp"),
            P("expert", None, "fsdp"),
            P("expert", "fsdp", None),
        ),
        out_specs=(
            P("expert", None),
            P("expert", None),
            P("expert", None),
            P("expert", None, "fsdp"),
            P("expert", None, "fsdp"),
            P("expert", "fsdp", None),
        ),
        check_vma=False,
    )
```

time: 96.5 us -> 88.1 us (0.913)
  Pallas kernels: 95.6 us -> 87.2 us
    pallas_call x1, Pallas kernels: 92.9 us -> 84 us  [per_device(): pl.pallas_call(kernel, out_shape=(pltpu.VMEM((2, NQ, NZ, TOK, QC), BF16),...]
where the time goes in v4:
time: 88.1 us; the launch traced here: 88 us
  Pallas kernels  87.2 us (99%)
    pallas_call x1, Pallas kernels, per_device(): pl.pallas_call(kernel, out_shape=(pltpu.VMEM((2, NQ, NZ, TOK, QC), BF16),...  84 us
    pallas_call x1, Pallas kernels, per_device(): pl.pallas_call(store, out_shape=(jax.ShapeDtypeStruct((TOK, D), BF16), ja...  3.15 us

profile of v4, /device:TPU:1, one launch (start us, length us, event | category | flops | bytes accessed | tf_op | source)
XLA Modules:
  0.0 88.0 jit_solution(10870768866167528155)
XLA Ops:
  0.6 84.0 %shard_map.118 = (bf16[2,3,8,128,128]{4,3,2,1,0:T(8,128)(2,1)S(1)}, f32[2,128]{1,0:T(2,128)S(1)}, bf16[3072,256]{1,0:T(8,128)(2,1)S(1)}, bf16[3072,256]{1,0:T(8,128)(2,1)S(1)}, bf16[256,3072]{1,0:T(8,128)(2,1)S(1)}) custom-call(bf16[128,3072]{1,0:T(8,128)(2,1)} %tokens.1, s32[2,128]{1,0:T(2,128)} %bitcast.3, f32[2,128]{1,0:T(2,128)} %bitcast.4, ...), custom_call_target="tpu_custom_call" | custom-call | tf_op jit(solution)/shard_map/pallas_call | solution.py:565
  84.7 3.2 %shard_map.119 = (bf16[128,3072]{1,0:T(8,128)(2,1)}, bf16[128,3072]{1,0:T(8,128)(2,1)}, f32[2,128]{1,0:T(2,128)}, bf16[1,3072,256]{2,1,0:T(8,128)(2,1)}, bf16[1,...) custom-call(bf16[2,3,8,128,128]{4,3,2,1,0:T(8,128)(2,1)S(1)} %get-tuple-element.17.outs, ...), custom_call_target="tpu_custom_call" | custom-call | tf_op jit(solution)/shard_map/pallas_call | solution.py:606

commit v5 on v4

--- a/solution.py
+++ b/solution.py
@@ -35,10 +35,10 @@
     tokens, assign_t, weight_t, cotangent, w_gate, w_up, w_down,
     outs, prob, gg, gu, gd,
     acts, cot_part, wgu, wd, send_x, send_y, xg, yd, acc_gu, acc_h, hid, gpre,
-    part, rp, rm, rc, gp, gp_sum,
+    part, rp, rm, rc, yx, gp, gp_sum,
     load_sem, wpre_sem,
     a_send, a_recv, d_send, d_recv, ring_send, ring_recv, sib_send, sib_recv, dsib_send, dsib_recv,
-    act_sem, rs_send, rs_recv, c_send, c_recv, o_send, o_recv, osib_send, osib_recv, g_send, g_recv, gsum_sem,
+    act_sem, yx_send, yx_recv, rs_send, rs_recv, c_send, c_recv, o_send, o_recv, osib_send, osib_recv, g_send, g_recv, gsum_sem,
 ):
     e = lax.axis_index("expert")
     f = lax.axis_index("fsdp")
@@ -116,9 +116,6 @@
     mine_u = rows_of(core + 2, H)
     land = (rp, rm)
 
-    def half(h):
-        return slice(h * HALF, (h + 1) * HALF)
-
     def target(way, s):
         return zmod(z + 4 - s) if way == 0 else zmod(z - 4 + s)
 
@@ -311,6 +308,19 @@
         probs = []
 
         def back(q):
+            shared = q == NQ - 1
+
+            def half(h):
+                if shared:
+                    return pl.ds(pl.multiple_of(yh * HALF + h * (HALF // 2), HALF // 2), HALF // 2)
+                return slice(h * HALF, (h + 1) * HALF)
+
+            def add_other(zd, d):
+                if shared:
+                    mine = rows_of(yh, HALF)
+                    arrived(yx.at[zd], yx_send.at[d % NZ], yx_recv.at[d % NZ])
+                    part[q, zd, mine, :] = (part[q, zd, mine, :].astype(F32) + yx[zd].astype(F32)).astype(BF16)
+
             def rs_start(way, s, h):
                 send(
                     part.at[q, target(way, s), half(h), :], land[way].at[q, s, half(h), :],
@@ -326,15 +336,26 @@
                     part[q, zd, half(h), :].astype(F32) + land[way][q, s, half(h), :].astype(F32)
                 ).astype(BF16)
 
+            if shared:
+                for d in (4, 3, 5, 2, 6, 1, 7, 0):
+                    zd = zmod(z + d)
+                    send(
+                        part.at[q, zd, rows_of(1 - yh, HALF), :], yx.at[zd],
+                        yx_send.at[d], yx_recv.at[d], dev(e, 1 - yh, z, core),
+                    )
+                yield
             if q == 0:
                 term(zmod(z + 4))
+            add_other(zmod(z + 4), 4)
             rs_start(0, 0, 0)
             rs_start(1, 0, 1)
             if q == 0:
                 term(zmod(z + 3))
+            add_other(zmod(z + 3), 3)
             rs_start(0, 1, 1)
             if q == 0:
                 term(zmod(z + 5))
+            add_other(zmod(z + 5), 5)
             rs_start(1, 1, 0)
             yield
             for way, h in ((0, 0), (1, 1)):
@@ -343,11 +364,14 @@
                 rs_start(way, 1, h)
             yield
             for s in (1, 2):
+                add_other(zmod(z + 3 - s), 3 - s)
+                add_other(zmod(z + 5 + s), 5 + s)
                 for way, h in ((0, 1), (1, 0), (0, 0), (1, 1)):
                     rs_arrived(way, s, h)
                     rs_add(way, s, h)
                     rs_start(way, s + 1, h)
                 yield
+            add_other(z, 0)
             for h in range(2):
                 for way in range(2):
                     rs_arrived(way, 3, h)
@@ -356,34 +380,78 @@
                     + rp[q, 3, half(h), :].astype(F32)
                     + rm[q, 3, half(h), :].astype(F32)
                 ).astype(BF16)
-            rc[q, yh, own_rows, :] = part[q, z, own_rows, :]
-            for i in range(E):
-                for dy in range(2):
-                    if i or dy:
-                        b = lax.rem(e + i, E)
-                        send(
-                            part.at[q, z, rows_of(b, CAP), :], rc.at[q, yh, own_rows, :],
-                            c_send.at[q, i * 2 + dy], c_recv.at[q, i * 2 + dy],
-                            dev(b, lax.rem(yh + dy, 2), z, core),
-                        )
-            yield
-            for i in range(E):
-                for dy in range(2):
-                    if i or dy:
-                        src = rows_of(lax.rem(e + E - i, E), CAP)
-                        arrived(
-                            rc.at[q, lax.rem(yh + dy, 2), src, :],
-                            c_send.at[q, i * 2 + dy], c_recv.at[q, i * 2 + dy],
-                        )
-            summed = (rc[q, 0].astype(F32) + rc[q, 1].astype(F32)).astype(BF16)
+            if shared:
+                def give(i, dy):
+                    b = yh * 4 + lax.rem(ex + i, 4)
+                    return remote(
+                        part.at[q, z, rows_of(b, CAP), :], rc.at[q, 0, own_rows, :],
+                        c_send.at[q, i * 2 + dy], c_recv.at[q, i * 2 + ey], dev(b, lax.rem(yh + dy, 2), z, core),
+                    )
+
+                @pl.when(yh == ey)
+                def _():
+                    rc[q, 0, own_rows, :] = part[q, z, own_rows, :]
+
+                @pl.when(yh != ey)
+                def _():
+                    give(0, 0).start()
+
+                for i in range(4):
+                    for dy in range(2):
+                        if i or dy:
+                            c = give(i, dy)
+                            c.start()
+                            pending.append(c)
+            else:
+                rc[q, yh, own_rows, :] = part[q, z, own_rows, :]
+                for i in range(E):
+                    for dy in range(2):
+                        if i or dy:
+                            b = lax.rem(e + i, E)
+                            send(
+                                part.at[q, z, rows_of(b, CAP), :], rc.at[q, yh, own_rows, :],
+                                c_send.at[q, i * 2 + dy], c_recv.at[q, i * 2 + dy],
+                                dev(b, lax.rem(yh + dy, 2), z, core),
+                            )
+            yield
+            if shared:
+                for i in range(4):
+                    for side in range(2):
+                        src = rc.at[q, 0, rows_of(side * 4 + lax.rem(ex + 4 - i, 4), CAP), :]
+                        if i:
+                            arrived(src, c_send.at[q, i * 2 + side], c_recv.at[q, i * 2 + side])
+                        else:
+
+                            @pl.when(jnp.logical_or(yh != ey, ey != side))
+                            def _(src=src, side=side):
+                                arrived(src, c_send.at[q, side], c_recv.at[q, side])
+
+                @pl.when(yh != ey)
+                def _():
+                    give(0, 0).wait_send()
+
+                summed = rc[q, 0]
+            else:
+                for i in range(E):
+                    for dy in range(2):
+                        if i or dy:
+                            src = rows_of(lax.rem(e + E - i, E), CAP)
+                            arrived(
+                                rc.at[q, lax.rem(yh + dy, 2), src, :],
+                                c_send.at[q, i * 2 + dy], c_recv.at[q, i * 2 + dy],
+                            )
+                summed = (rc[q, 0].astype(F32) + rc[q, 1].astype(F32)).astype(BF16)
             out0 = jnp.dot(pick0, summed, preferred_element_type=F32)
             out1 = jnp.dot(pick1, summed, preferred_element_type=F32)
             mixed = w0 * out0 + w1 * out1 if t == 0 else out0 + out1
-            outs[t, q, z] = mixed.astype(BF16)
+            outs[t, :, pl.ds(pl.multiple_of(z * RS + q * QC, QC), QC)] = mixed.astype(BF16)
+
+            def columns(zz):
+                return pl.ds(pl.multiple_of(zz * RS + q * QC, QC), QC)
 
             def view(kind, zz, h=None):
                 rows = slice(0, TOK) if h is None else slice(h * (TOK // 2), (h + 1) * (TOK // 2))
-                return outs.at[kind, q, zz, rows, :]
+                return outs.at[kind, rows, columns(zz)]
 
             sems = (o_send.at[q], o_recv.at[q], osib_send.at[q], osib_recv.at[q])
             steps = spread_out(view, sems)
@@ -494,23 +562,15 @@
             arrived(gpre.at[:, 2 * H : 3 * H], act_sem.at[1], act_sem.at[3])
         go(q0, q1)
         other_terms()
-        go(q0, q2)
+        go(q2, q0, q1)
         weight_grads(0)
-        go(q0, q1)
+        go(q0, q1, q2)
         weight_grads(1)
-        go(q0, q1, q2)
+        go(q0, q1, q2, q0, q2, q1, q2, q0, q2)
         weight_grads(2)
-        go(q0, q1, q2)
+        go(q1, q0, q2)
         weight_grads(3)
-        go(q1, q2)
-        go(q0)
-        go(q2)
-        go(q1, q0)
-        go(q0, q1)
-        go(q2)
-        go(q1)
-        go(q2)
-        go(q2)
+        go(q1, q2, q0, q1)
         if t == 0:
             for dz in range(1, NZ):
                 arrived(gp.at[zmod(z - dz)], g_send.at[dz], g_recv.at[dz])
@@ -519,7 +579,8 @@
                 total = total + gp[zz]
             gp_sum[...] = total
             send(gp_sum, gp_sum, gsum_sem.at[0], gsum_sem.at[1], sibling)
-        else:
+        go(q2)
+        if t == 1:
             arrived(gp_sum, gsum_sem.at[0], gsum_sem.at[1])
         go(q0, q1, q2)
 
@@ -538,22 +599,13 @@
 
 def store(outs, prob, gg, gu, gd, moe_out, grad_tokens, grad_prob, grad_gate, grad_up, grad_down, sem):
     copies = []
-
-    def copy(src, dst, i):
-        c = pltpu.make_async_copy(src, dst, sem.at[i])
+    for i, (src, dst) in enumerate((
+        (gg, grad_gate.at[0]), (gu, grad_up.at[0]), (gd, grad_down.at[0]),
+        (outs.at[0], moe_out), (outs.at[1], grad_tokens), (prob, grad_prob),
+    )):
+        copies.append(pltpu.make_async_copy(src, dst, sem.at[i]))
+    for c in copies:
         c.start()
-        copies.append(c)
-
-    for kind, dst in enumerate((moe_out, grad_tokens)):
-        for q in range(NQ):
-            for zz in range(NZ):
-                columns = slice(zz * RS + q * QC, zz * RS + (q + 1) * QC)
-                copy(outs.at[kind, q, zz], dst.at[:, columns], (kind * NQ + q) * NZ + zz)
-    first = 2 * NQ * NZ
-    copy(gg, grad_gate.at[0], first)
-    copy(gu, grad_up.at[0], first + 1)
-    copy(gd, grad_down.at[0], first + 2)
-    copy(prob, grad_prob, first + 3)
     for c in copies:
         c.wait()
 
@@ -565,7 +617,7 @@
     held = pl.pallas_call(
         kernel,
         out_shape=(
-            pltpu.VMEM((2, NQ, NZ, TOK, QC), BF16),
+            pltpu.VMEM((2, TOK, D), BF16),
             pltpu.VMEM((2, TOK), F32),
             pltpu.VMEM((D, H), BF16),
             pltpu.VMEM((D, H), BF16),
@@ -590,12 +642,13 @@
             pltpu.VMEM((NQ, 4, SLOTS, QC), BF16),
             pltpu.VMEM((NQ, 4, SLOTS, QC), BF16),
             pltpu.VMEM((NQ, 2, SLOTS, QC), BF16),
+            pltpu.VMEM((NZ, HALF, QC), BF16),
             pltpu.VMEM((NZ, 8, TOK), F32),
             pltpu.VMEM((8, TOK), F32),
             dma((5 + NG,)), dma((4,)),
             dma((E - 1,)), dma((E - 1,)), dma((NG, E - 1)), dma((NG, E - 1)),
             dma((2, 4, NP)), dma((2, 4, NP)), dma((NZ, NP)), dma((NZ, NP)), dma((NG,)), dma((NG,)),
-            dma((4,)), dma((NQ, 8, 2)), dma((NQ, 8, 2)), dma((NQ, 2 * E)), dma((NQ, 2 * E)),
+            dma((4,)), dma((NZ,)), dma((NZ,)), dma((NQ, 8, 2)), dma((NQ, 8, 2)), dma((NQ, 2 * E)), dma((NQ, 2 * E)),
             dma((NQ, 8)), dma((NQ, 8)), dma((NQ, NZ + 1)), dma((NQ, NZ + 1)),
             dma((NZ,)), dma((NZ,)), dma((2,)),
         ],
@@ -615,7 +668,7 @@
         ),
         in_specs=[vmem] * 5,
         out_specs=(hbm,) * 6,
-        scratch_shapes=[dma((2 * NQ * NZ + 4,))],
+        scratch_shapes=[dma((6,))],
         compiler_params=pltpu.CompilerParams(vmem_limit_bytes=16 * 1024 * 1024),
     )(*held)
     return (moe_out, grad_tokens, grad_prob.T, grad_gate, grad_up, grad_down)

time: 88.1 us -> 83.3 us (0.946)
  Pallas kernels: 87.2 us -> 82.4 us
    pallas_call x1, Pallas kernels: 84 us -> 79.7 us  [per_device(): pl.pallas_call(kernel, out_shape=(pltpu.VMEM((2, TOK, D), BF16), pltpu.VM...]
where the time goes in v5:
time: 83.3 us; the launch traced here: 83.2 us
  Pallas kernels  82.4 us (99%)
    pallas_call x1, Pallas kernels, per_device(): pl.pallas_call(kernel, out_shape=(pltpu.VMEM((2, TOK, D), BF16), pltpu.VM...  79.7 us
    pallas_call x1, Pallas kernels, per_device(): pl.pallas_call(store, out_shape=(jax.ShapeDtypeStruct((TOK, D), BF16), ja...  2.73 us

profile of v5, /device:TPU:1, one launch (start us, length us, event | category | flops | bytes accessed | tf_op | source)
XLA Modules:
  0.0 83.2 jit_solution(17154029802663459873)
XLA Ops:
  0.6 79.7 %shard_map.118 = (bf16[2,128,3072]{2,1,0:T(8,128)(2,1)S(1)}, f32[2,128]{1,0:T(2,128)S(1)}, bf16[3072,256]{1,0:T(8,128)(2,1)S(1)}, bf16[3072,256]{1,0:T(8,128)(2,1)S(1)}, bf16[256,3072]{1,0:T(8,128)(2,1)S(1)}) custom-call(bf16[128,3072]{1,0:T(8,128)(2,1)} %tokens.1, s32[2,128]{1,0:T(2,128)} %bitcast.3, f32[2,128]{1,0:T(2,128)} %bitcast.4, ...), custom_call_target="tpu_custom_call" | custom-call | tf_op jit(solution)/shard_map/pallas_call | solution.py:617
  80.3 2.7 %shard_map.119 = (bf16[128,3072]{1,0:T(8,128)(2,1)}, bf16[128,3072]{1,0:T(8,128)(2,1)}, f32[2,128]{1,0:T(2,128)}, bf16[1,3072,256]{2,1,0:T(8,128)(2,1)}, bf16[1,...) custom-call(bf16[2,128,3072]{2,1,0:T(8,128)(2,1)S(1)} %get-tuple-element.17.outs, ...), custom_call_target="tpu_custom_call" | custom-call | tf_op jit(solution)/shard_map/pallas_call | solution.py:659

commit v6 on v5

--- a/solution.py
+++ b/solution.py
@@ -566,11 +566,11 @@
         weight_grads(0)
         go(q0, q1, q2)
         weight_grads(1)
-        go(q0, q1, q2, q0, q2, q1, q2, q0, q2)
+        go(q0, q1, q2, q0, q2, q1, q2, q0, q2, q1)
         weight_grads(2)
-        go(q1, q0, q2)
+        go(q0, q2, q1)
         weight_grads(3)
-        go(q1, q2, q0, q1)
+        go(q2, q0, q1)
         if t == 0:
             for dz in range(1, NZ):
                 arrived(gp.at[zmod(z - dz)], g_send.at[dz], g_recv.at[dz])

time: 83.3 us -> 82.8 us (level)
  no operation moved by 1% of the time
where the time goes in v6:
time: 82.8 us; the launch traced here: 82.7 us
  Pallas kernels  81.8 us (99%)
    pallas_call x1, Pallas kernels, per_device(): pl.pallas_call(kernel, out_shape=(pltpu.VMEM((2, TOK, D), BF16), pltpu.VM...  79.1 us
    pallas_call x1, Pallas kernels, per_device(): pl.pallas_call(store, out_shape=(jax.ShapeDtypeStruct((TOK, D), BF16), ja...  2.73 us

profile of v6, /device:TPU:1, one launch (start us, length us, event | category | flops | bytes accessed | tf_op | source)
XLA Modules:
  0.0 82.7 jit_solution(17995371199740403336)
XLA Ops:
  0.6 79.1 %shard_map.118 = (bf16[2,128,3072]{2,1,0:T(8,128)(2,1)S(1)}, f32[2,128]{1,0:T(2,128)S(1)}, bf16[3072,256]{1,0:T(8,128)(2,1)S(1)}, bf16[3072,256]{1,0:T(8,128)(2,1)S(1)}, bf16[256,3072]{1,0:T(8,128)(2,1)S(1)}) custom-call(bf16[128,3072]{1,0:T(8,128)(2,1)} %tokens.1, s32[2,128]{1,0:T(2,128)} %bitcast.3, f32[2,128]{1,0:T(2,128)} %bitcast.4, ...), custom_call_target="tpu_custom_call" | custom-call | tf_op jit(solution)/shard_map/pallas_call | solution.py:617
  79.8 2.7 %shard_map.119 = (bf16[128,3072]{1,0:T(8,128)(2,1)}, bf16[128,3072]{1,0:T(8,128)(2,1)}, f32[2,128]{1,0:T(2,128)}, bf16[1,3072,256]{2,1,0:T(8,128)(2,1)}, bf16[1,...) custom-call(bf16[2,128,3072]{2,1,0:T(8,128)(2,1)S(1)} %get-tuple-element.17.outs, ...), custom_call_target="tpu_custom_call" | custom-call | tf_op jit(solution)/shard_map/pallas_call | solution.py:659
